TPU v7x, 128 devices: a whole 4x4x4 slice. The times are simulated.
128 devices in a mesh: dir: 2 (over x_lo), shard: 64 (over x_hi, y, z, core).
Axes of the slice: x: 4 (x_hi: 2, x_lo: 2; x = x_hi * 2 + x_lo), y: 4, z: 4, core: 2. Of those that a mesh axis runs over, the one named last changes fastest.
Arguments:
- propagators: bfloat16 [2, 512, 64, 1024], P('dir', 'shard'), may hold values from 0.5 to 1.5
- field: float32 [64, 1024], replicated, may hold values from -0.5 to 0.5
- orient: float32 [3, 512], replicated, may hold values from -1 to 1, as said below
- quad_weights: float32 [512], replicated, may hold values from 0.01 to 0.1
- analysis: bfloat16 [441, 512], replicated, may hold values from -0.25 to 0.25
- synthesis: bfloat16 [512, 441], replicated, may hold values from -0.4375 to 0.4375
- decay: float32 [441], replicated, may hold values from 0.5 to 1
Outputs:
- density: float32 [64, 1024], P('shard', 'dir')
- qtensor: float32 [5, 64, 1024], P(None, 'shard', 'dir')
Inputs may be any that keep to these rules, and one draw needn't show every extreme that they name: Each column of orient is a unit vector.
All inputs are finite; a program needn't handle non-finite values.
Results may differ from a plain program's by a relative error of at most 0.028.
Values may be sent and summed in bfloat16 or wider, within the bound.
No kernel may reach another device: no remote copies, remote signals or barrier semaphores. Data moves between devices by JAX's collectives and lax.ppermute only.
A program may use at most 128 MiB of HBM per device.

v0:
```python
import functools
import math

import jax
import jax.numpy as jnp
import numpy as np
from jax import lax
from jax.experimental import pallas as pl
from jax.experimental.pallas import tpu as pltpu
from jax.sharding import PartitionSpec as P

NX = 64
NY = 64
NZ = 16
M = 512
CELLS = NY * NZ
SHARDS = 64
LOCAL = M // SHARDS
TRANSPORT = 1.5
THIRD = 1.0 / 3.0
BF = jnp.bfloat16
F32 = jnp.float32
NYQUIST_ROWS = 80
VMEM_LIMIT = 56 * 1024 * 1024


def slot_list():
    plain, nyquist = [], []
    for kz in range(1, 8):
        for ky in range(64):
            (nyquist if ky == 32 else plain).append(((ky, kz), (ky, kz), True))
    for ky in range(1, 32):
        plain.append(((ky, 0), (ky, 0), True))
        nyquist.append(((ky, 8), (ky, 8), True))
    nyquist.append(((0, 0), (0, 8), False))
    nyquist.append(((32, 0), (32, 8), False))
    return plain + nyquist


def point_waves(point):
    ky, kz = point
    fy = ky if ky <= 31 else ky - 64
    fz = kz if kz <= 7 else kz - 16
    rest = (0.0 if ky == 32 else fy / 64.0, 0.0 if kz == 8 else fz / 16.0)
    nyq = (-0.5 if ky == 32 else 0.0, -0.5 if kz == 8 else 0.0)
    return rest, nyq


@functools.lru_cache(maxsize=None)
def tables():
    slots = slot_list()
    y = np.arange(64)[:, None]
    z = np.arange(16)[None, :]
    forward = np.zeros((64, 2, 8, CELLS))
    weight = np.zeros((64, 2, 8))
    waves = np.zeros((8, 512), np.float32)
    for at, (re_point, im_point, paired) in enumerate(slots):
        group, slot = divmod(at, 8)
        for part, point in enumerate((re_point, im_point)):
            angle = 2.0 * math.pi * (((point[0] * y) % 64) / 64.0 + ((point[1] * z) % 16) / 16.0)
            row = -np.sin(angle) if (paired and part == 1) else np.cos(angle)
            forward[group, part, slot] = row.reshape(-1)
            weight[group, part, slot] = (2.0 if paired else 1.0) / CELLS
            rest, nyq = point_waves(point)
            waves[2 * part, at], waves[2 * part + 1, at] = rest
            waves[4 + 2 * part, at], waves[5 + 2 * part, at] = nyq
    forward = forward.reshape(1024, CELLS)
    weight = weight.reshape(1024)
    inverse = forward.T * weight[None, :]
    x = np.arange(64)[:, None]
    j = np.arange(32)[None, :]
    angle = 2.0 * math.pi * ((x * j) % 64) / 64.0
    cosine = np.cos(angle)
    sine = -np.sin(angle)
    partner_c, partner_s = sine.copy(), -cosine
    sine[:, 0] = (-1.0) ** np.arange(64)
    partner_s[:, 0] = 0.0
    partner_c[:, 0] = 0.0
    fx = np.concatenate([cosine, sine], 1)
    fx_partner = np.concatenate([partner_c, partner_s], 1)
    wx = np.full(64, 2.0 / 64)
    wx[0] = wx[32] = 1.0 / 64
    fx_inv = (fx * wx[None, :]).T
    return dict(forward=forward, inverse=inverse, waves=waves, fx=fx, fxp=fx_partner, fxi=fx_inv)


def turns_cos(t):
    return turns_sin(t + 0.25)


def turns_sin(t):
    r = t - jnp.round(t)
    r = jnp.where(r > 0.25, 0.5 - r, jnp.where(r < -0.25, -0.5 - r, r))
    v = r * (2.0 * math.pi)
    s = v * v
    p = -2.5052108e-8
    p = p * s + 2.7557319e-6
    p = p * s - 1.9841270e-4
    p = p * s + 8.3333333e-3
    p = p * s - 1.6666667e-1
    return v + v * s * p


def dot(a, b):
    return jnp.dot(a, b, preferred_element_type=F32)


def dot_nt(a, b):
    return lax.dot_general(a, b, (((1,), (1,)), ((), ())), preferred_element_type=F32)


def split2(v):
    hi = v.astype(BF)
    lo = (v - hi.astype(F32)).astype(BF)
    return hi, lo


def step_one_kernel(head_ref, q_ref, fwd_ref, inv_ref, field_ref, waves_ref, fx_ref, fxp_ref, fxi_ref, out_ref):
    head = head_ref[...]
    hx, hy, hz = head[:, 0:1], head[:, 1:2], head[:, 2:3]
    w = waves_ref[...]
    rest_re = hy * w[0:1] + hz * w[1:2]
    rest_im = hy * w[2:3] + hz * w[3:4]
    nyq_re = hy * w[4:5] + hz * w[5:6]
    nyq_im = hy * w[6:7] + hz * w[7:8]
    x_nyq = turns_sin(hx * -0.5)
    c_re, s_re, c_im = turns_cos(rest_re), turns_sin(rest_re), turns_cos(rest_im)
    cn_re, cn_im = turns_cos(nyq_re), turns_cos(nyq_im)
    sn_re, sn_im = turns_sin(nyq_re) * x_nyq, turns_sin(nyq_im) * x_nyq
    lane_m = lax.broadcasted_iota(jnp.int32, (8, 512), 1) // 64
    pick = (lax.broadcasted_iota(jnp.int32, (8, 512), 0) == lane_m).astype(BF)
    pick2 = jnp.concatenate([pick, pick], 0)

    def spread(tab):
        hi, lo = split2(tab.T)
        return dot(jnp.concatenate([hi, lo], 1), pick2)

    a = spread(c_re * cn_re).reshape(64, 8, 512)
    d = spread(c_im * cn_im).reshape(64, 8, 512)
    b = spread(s_re * cn_re).reshape(64, 8, 512)
    lane_j = lax.broadcasted_iota(jnp.int32, (8, 64), 1)
    freq = (lane_j % 32).astype(F32) * (1.0 / 64.0)
    is_nyq = lane_j == 32
    cx = jnp.where(is_nyq, turns_cos(hx * -0.5), turns_cos(hx * freq))
    sx = jnp.where(is_nyq, 0.0, turns_sin(hx * freq))
    rows = (fx_ref[...][None] * cx[:, None, :] + fxp_ref[...][None] * sx[:, None, :]).reshape(512, 64)
    hi, lo = split2(rows)
    inv8 = jnp.concatenate([fxi_ref[...]] * 8, 1)
    full = dot(hi, inv8) + dot(lo, inv8)
    row_m = lax.broadcasted_iota(jnp.int32, (512, 512), 0) // 64
    col_m = lax.broadcasted_iota(jnp.int32, (512, 512), 1) // 64
    same = row_m == col_m
    shift_x = jnp.where(same, full, 0.0).astype(BF)
    odd = (lax.broadcasted_iota(jnp.int32, (512, 512), 0) + lax.broadcasted_iota(jnp.int32, (512, 512), 1)) % 2
    nyq_x = jnp.where(same, jnp.where(odd == 1, 1.0 / 64, -1.0 / 64), 0.0).astype(BF)

    spec = dot_nt(fwd_ref[...], q_ref[...]).reshape(64, 2, 8, 512)
    re, im = spec[:, 0], spec[:, 1]
    u = jnp.stack([a * re + b * im, d * im - b * re], 1).reshape(1024, 512).astype(BF)
    ng = NYQUIST_ROWS // 16
    ta = spread(c_re * sn_re)[512 - 8 * ng :].reshape(ng, 8, 512)
    td = spread(c_im * sn_im)[512 - 8 * ng :].reshape(ng, 8, 512)
    tb = spread(s_re * sn_re)[512 - 8 * ng :].reshape(ng, 8, 512)
    ret, imt = re[64 - ng :], im[64 - ng :]
    tail = jnp.stack([ta * ret + tb * imt, td * imt - tb * ret], 1).reshape(NYQUIST_ROWS, 512).astype(BF)
    head_rows = dot(u[: 1024 - NYQUIST_ROWS], shift_x).astype(BF)
    tail_rows = (dot(u[1024 - NYQUIST_ROWS :], shift_x) + dot(tail, nyq_x)).astype(BF)
    turned = jnp.concatenate([head_rows, tail_rows], 0)
    damp = jnp.exp(-field_ref[...])
    damp = jnp.concatenate([damp, damp], 0).T
    damp = jnp.concatenate([damp] * 4, 1)
    moved = (dot(inv_ref[...], turned) * damp).astype(BF)
    out_ref[...] = dot(fwd_ref[...], moved).astype(BF).reshape(64, 16, 512)


def mix_kernel(head_ref, x_ref, d_ref, waves_ref, fx_ref, fxp_ref, fxi_ref, out_ref, wide_ref, mixed_ref):
    for quad in range(4):
        wide_ref[pl.ds(quad * 1024, 1024), :] = (
            x_ref[:, :, quad * 128 : (quad + 1) * 128].reshape(1024, 128).astype(F32)
        )
    left = lax.broadcasted_iota(jnp.int32, (64, 128), 1) < 64
    for pair in range(8):
        for quad in range(4):
            first = wide_ref[pl.ds(quad * 1024 + 2 * pair, 64, stride=16), :]
            second = wide_ref[pl.ds(quad * 1024 + 2 * pair + 1, 64, stride=16), :]
            even = jnp.where(left, first, pltpu.roll(second, 64, 1))
            odd = jnp.where(left, pltpu.roll(first, 64, 1), second)
            mixed_ref[pl.ds(2 * quad * 64, 64), pl.ds(pair * 128, 128)] = even.astype(BF)
            mixed_ref[pl.ds((2 * quad + 1) * 64, 64), pl.ds(pair * 128, 128)] = odd.astype(BF)
    dmat = d_ref[...]
    row = lax.broadcasted_iota(jnp.int32, (512, 512), 0)
    col = lax.broadcasted_iota(jnp.int32, (512, 512), 1)
    perm = ((row % 8) * 64 + row // 8 == col).astype(BF)
    d_first = dot(dmat, perm).astype(BF)
    mixed = dot(d_first, mixed_ref[...]).astype(BF)
    head = head_ref[...]
    hx, hy, hz = head[:, 0:1], head[:, 1:2], head[:, 2:3]
    lane = lax.broadcasted_iota(jnp.int32, (512, 128), 1) % 64
    freq = (lane % 32).astype(F32) * (1.0 / 64.0)
    is_nyq = lane == 32
    cx = jnp.where(is_nyq, 1.0, turns_cos(hx * freq))
    sx = jnp.where(is_nyq, 0.0, turns_sin(hx * freq))
    w = waves_ref[...]
    rest = hy * w[0:1] + hz * w[1:2]
    nyq = hx * w[4:5] + hy * w[2:3] + hz * w[3:4]
    cn = turns_cos(nyq)
    tc = turns_cos(rest) * cn
    ts = turns_sin(rest) * cn
    src = lax.broadcasted_iota(jnp.int32, (256, 512), 0) % 128
    dst = lax.broadcasted_iota(jnp.int32, (256, 512), 1)
    want = jnp.where(dst % 64 == 32, 16, 0) + dst // 64
    pick_re = (src == want).astype(BF)
    pick_im = (src == want + 8).astype(BF)
    tc2 = jnp.concatenate(split2(tc), 1)
    ts2 = jnp.concatenate(split2(ts), 1)
    a = dot(tc2, pick_re)
    d = dot(tc2, pick_im)
    b = dot(ts2, pick_re)
    cx = jnp.concatenate([cx] * 2, 1)
    sx = jnp.concatenate([sx] * 2, 1)
    parts = []
    for block in range(4):
        piece = mixed[:, block * 256 : (block + 1) * 256]
        parts.append(cx * dot(piece, fx_ref[...]) + sx * dot(piece, fxp_ref[...]))
    re = jnp.concatenate(parts[:2], 1)
    im = jnp.concatenate(parts[2:], 1)
    turned = jnp.concatenate([a * re + b * im, d * im - b * re], 1).astype(BF)
    last = dot(dmat, turned).astype(BF)
    out = dot_nt(fxi_ref[...], last).astype(BF).reshape(64, 16, 512)
    out_ref[0] = out[:, :, :256]
    out_ref[1] = out[:, :, 256:]


def moment_kernel(dir_ref, x_ref, inv_ref, field_ref, orient_ref, weight_ref, keep_ref, send_ref):
    first = dot(inv_ref[...], x_ref[0])
    second = dot(inv_ref[...], x_ref[1])
    hi, lo = split2(first * second)
    o = orient_ref[...]
    ux, uy, uz = o[0:1], o[1:2], o[2:3]
    rows = [jnp.ones_like(ux), ux * ux - THIRD, uy * uy - THIRD, ux * uy, ux * uz, uy * uz, 0.0 * ux, 0.0 * ux]
    g_hi, g_lo = split2(jnp.concatenate(rows, 0) * weight_ref[...])
    result = dot_nt(g_hi, hi) + dot_nt(g_hi, lo) + dot_nt(g_lo, hi)
    damp = jnp.exp(-field_ref[...])
    result = result * (damp * damp)
    is_first = dir_ref[0] == 0
    keep_ref[...] = jnp.where(is_first, result[:, :512], result[:, 512:])
    send_ref[...] = jnp.where(is_first, result[:, 512:], result[:, :512])


def group_waves(waves):
    table = np.zeros((64, 8, 128), np.float32)
    for group in range(64):
        cols = slice(group * 8, group * 8 + 8)
        for flag in range(2):
            for role in range(2):
                at = slice(flag * 16 + role * 8, flag * 16 + role * 8 + 8)
                table[group, 0, at] = waves[2 * role, cols]
                table[group, 1, at] = waves[2 * role + 1, cols]
                table[group, 2, at] = waves[4 + 2 * role, cols]
                table[group, 3, at] = waves[5 + 2 * role, cols]
                table[group, 4, at] = -0.5 * flag
    return table


def call(kernel, out_shape, args, scratch=(), smem_first=False):
    specs = [pl.BlockSpec(memory_space=pltpu.VMEM) for _ in args]
    if smem_first:
        specs[0] = pl.BlockSpec(memory_space=pltpu.SMEM)
    return pl.pallas_call(
        kernel,
        out_shape=out_shape,
        in_specs=specs,
        out_specs=jax.tree.map(lambda _: pl.BlockSpec(memory_space=pltpu.VMEM), out_shape),
        scratch_shapes=list(scratch),
        compiler_params=pltpu.CompilerParams(vmem_limit_bytes=VMEM_LIMIT),
    )(*args)


def on_device(propagators, field, orient, quad_weights, analysis, synthesis, decay):
    tab = tables()
    forward = jnp.asarray(tab["forward"].astype(BF))
    inverse = jnp.asarray(tab["inverse"].astype(BF))
    fx = jnp.asarray(tab["fx"].astype(np.float32))
    fxp = jnp.asarray(tab["fxp"].astype(np.float32))
    fxi = jnp.asarray(tab["fxi"].astype(BF))
    eye4 = np.eye(4)
    fx4 = jnp.asarray(np.kron(eye4, tab["fx"]).astype(BF))
    fxp4 = jnp.asarray(np.kron(eye4, tab["fxp"]).astype(BF))
    inv_x = np.zeros((64, 16, 16, 64))
    for r in range(16):
        inv_x[:, r, r, :] = tab["fxi"].T
    inv_x = jnp.asarray(inv_x.reshape(1024, 1024).astype(BF))
    shard = lax.axis_index("shard")
    direction = lax.axis_index("dir")
    heading = (orient * (TRANSPORT * (1.0 - 2.0 * direction.astype(F32)))).T
    local_heading = lax.dynamic_slice_in_dim(heading, shard * LOCAL, LOCAL, 0)
    state = propagators.reshape(LOCAL * NX, CELLS)
    first = call(
        step_one_kernel,
        jax.ShapeDtypeStruct((64, 16, 512), BF),
        (local_heading, state, forward, inverse, field, jnp.asarray(tab["waves"]), fx, fxp, fxi),
    )
    d_matrix = jnp.dot(
        synthesis, (analysis.astype(F32) * decay[:, None]).astype(BF), preferred_element_type=F32
    ).astype(BF)
    gathered = lax.all_to_all(first, "shard", split_axis=0, concat_axis=0, tiled=True)
    local_waves = lax.dynamic_index_in_dim(jnp.asarray(group_waves(tab["waves"])), shard, 0, False)
    mixed = call(
        mix_kernel,
        jax.ShapeDtypeStruct((2, 64, 16, 256), BF),
        (heading, gathered, d_matrix, local_waves, fx4, fxp4, inv_x),
        (pltpu.VMEM((4096, 128), F32), pltpu.VMEM((512, 1024), BF)),
    )
    planes = lax.all_to_all(
        mixed.reshape(128, 16, 256), ("dir", "shard"), split_axis=0, concat_axis=0, tiled=True
    ).reshape(2, 1024, 256)
    local_field = lax.dynamic_slice_in_dim(field, shard, 1, 0)
    half_orient = lax.dynamic_slice_in_dim(orient, direction * 256, 256, 1)
    half_weight = lax.dynamic_slice_in_dim(quad_weights, direction * 256, 256, 0)[None]
    keep, send = call(
        moment_kernel,
        (jax.ShapeDtypeStruct((8, 512), F32), jax.ShapeDtypeStruct((8, 512), F32)),
        (direction[None].astype(jnp.int32), planes, inverse, local_field, half_orient, half_weight),
        smem_first=True,
    )
    total = keep + lax.ppermute(send, "dir", [(0, 1), (1, 0)])
    return total[:1], total[1:6, None]


def solution(mesh):
    in_specs = (P("dir", "shard", None, None), P(), P(), P(), P(), P(), P())
    out_specs = (P("shard", "dir"), P(None, "shard", "dir"))
    return jax.shard_map(on_device, mesh=mesh, in_specs=in_specs, out_specs=out_specs, check_vma=False)
```

profile of v0, /device:TPU:0, one launch (start us, length us, event | category | flops | bytes accessed | tf_op | source)
XLA Modules:
  0.0 85.8 jit_solution(11005047627270102641)
XLA Ops:
  0.6 0.0 copy-start
  0.7 0.9 %copy.19 = f32[3,512]{0,1:T(8,128)S(1)} copy(f32[3,512]{1,0:T(4,128)} %param.19) | data formatting | bytes 12288 | tf_op args[2]
  1.6 0.6 dynamic-slice_bitcast_fusion.1.head_ref
  2.2 9.2 %shard_map.176 = bf16[64,16,512]{2,1,0:T(8,128)(2,1)} custom-call(f32[8,3]{1,0:T(8,128)} %dynamic-slice_bitcast_fusion.1.head_ref, bf16[512,1024]{1,0:T(8,128)(2,1)} %bitcast.18, bf16[1024,1024]{1,0:T(8,128)(2,1)} %constant.49.clone.fwd_ref, bf16[1024,1024]{1,0:T(8,128)(2,1)} %constant.50.clone.inv_ref, f32[64,1024]{1,0:T(8,128)} %field_ref.1, ...), custom_call_target="tpu_custom_call" | custom-call | tf_op jit(solution)/shard_map/pallas_call | solution.py:269
  11.4 0.0 copy-start.5
  11.4 0.0 copy-start.6
  11.4 11.6 %all-to-all-start = ((bf16[64,16,512]{2,1,0:T(8,128)(2,1)}), bf16[64,16,512]{2,1,0:T(8,128)(2,1)S(1)}, u32[]{:S(2)}, u32[]{:S(2)}) async-start(bf16[64,16,512]{2,1,0:T(8,128)(2,1)} %shard_map.176), calls=%async_computation | async-start | bytes 2097152 | tf_op jit(solution)/shard_map/all_to_all | solution.py:306
  23.0 1.3 %dynamic-slice_bitcast_fusion.waves_ref = f32[8,128]{1,0:T(8,128)} fusion(f32[64,8,128]{2,1,0:T(8,128)} %constant.58.clone, s32[]{:T(128)S(6)} %select_n.13), kind=kLoop, calls=%fused_computation.6 | loop fusion | bytes 8196 | tf_op jit(solution)/shard_map/jit(dynamic_index_in_dim)/squeeze | solution.py:307
  24.3 0.7 fusion.3.head_ref
  25.0 0.0 copy-done
  25.0 0.0 copy-done.5
  25.0 0.0 copy-done.6
  25.1 1.4 %fusion.d_ref = bf16[512,512]{1,0:T(8,128)(2,1)} fusion(bf16[512,441]{0,1:T(8,128)(2,1)S(1)} %copy-done, bf16[441,512]{1,0:T(8,128)(2,1)S(1)} %copy-done.5, f32[441]{0:T(512)S(1)} %copy-done.6), kind=kOutput, calls=%fused_computation.1 | convolution fusion | flops 232150528 | bytes 1429220 | tf_op jit(solution)/shard_map/dot_general | solution.py:303
  26.4 14.7 %all-to-all-done.x_ref = bf16[64,16,512]{2,1,0:T(8,128)(2,1)S(1)} async-done(((bf16[64,16,512]{2,1,0:T(8,128)(2,1)}), bf16[64,16,512]{2,1,0:T(8,128)(2,1)S(1)}, u32[]{:S(2)}, u32[]{:S(2)}) %all-to-all-start) | async-done | bytes 1048608 | tf_op jit(solution)/shard_map/all_to_all | solution.py:306
  41.1 0.0 copy-start.2
  41.1 1.0 %copy-done.2 = bf16[64,16,512]{2,1,0:T(8,128)(2,1)} copy-done((bf16[64,16,512]{2,1,0:T(8,128)(2,1)}, bf16[64,16,512]{2,1,0:T(8,128)(2,1)S(1)}, u32[]{:S(2)}) %copy-start.2) | copy-done | bytes 1048600
  42.1 8.2 %shard_map.177 = bf16[2,64,16,256]{3,2,1,0:T(8,128)(2,1)} custom-call(f32[512,3]{1,0:T(8,128)} %fusion.3.head_ref, bf16[64,16,512]{2,1,0:T(8,128)(2,1)} %copy-done.2, bf16[512,512]{1,0:T(8,128)(2,1)} %fusion.d_ref, f32[8,128]{1,0:T(8,128)} %dynamic-slice_bitcast_fusion.waves_ref, bf16[256,256]{1,0:T(8,128)(2,1)} %constant.54.clone.fx_ref, ...), custom_call_target="tpu_custom_call" | custom-call | tf_op jit(solution)/shard_map/pallas_call | solution.py:269
  50.3 0.0 copy-start.4
  50.3 0.0 copy-start.3
  50.3 5.8 %all-to-all-start.1 = ((bf16[128,16,256]{2,1,0:T(8,128)(2,1)}), bf16[128,16,256]{2,1,0:T(8,128)(2,1)S(1)}, u32[]{:S(2)}, u32[]{:S(2)}) async-start(bf16[128,16,256]{2,1,0:T(8,128)(2,1)} %bitcast.17), calls=%async_computation.1 | async-start | bytes 2097152 | tf_op jit(solution)/shard_map/all_to_all | solution.py:314
  56.1 0.0 copy-done.4
  56.1 0.6 dynamic_slice.20
  56.7 0.0 copy-done.3
  56.7 0.6 constant_dynamic-slice_fusion.orient_ref
  57.3 1.4 %constant_dynamic-slice_fusion.1.field_ref = f32[1,1024]{1,0:T(1,128)} fusion(f32[64,1024]{1,0:T(8,128)} %field_ref.1, s32[]{:T(128)S(6)} %select_n.13), kind=kLoop, calls=%fused_computation.9 | loop fusion | bytes 8196 | tf_op jit(solution)/shard_map/dynamic_slice | solution.py:317
  58.7 16.1 %all-to-all-done.1 = bf16[128,16,256]{2,1,0:T(8,128)(2,1)S(1)} async-done(((bf16[128,16,256]{2,1,0:T(8,128)(2,1)}), bf16[128,16,256]{2,1,0:T(8,128)(2,1)S(1)}, u32[]{:S(2)}, u32[]{:S(2)}) %all-to-all-start.1) | async-done | bytes 1048608 | tf_op jit(solution)/shard_map/all_to_all | solution.py:314
  74.8 0.0 copy-start.1
  74.8 1.0 %copy-done.1 = bf16[128,16,256]{2,1,0:T(8,128)(2,1)} copy-done((bf16[128,16,256]{2,1,0:T(8,128)(2,1)}, bf16[128,16,256]{2,1,0:T(8,128)(2,1)S(1)}, u32[]{:S(2)}) %copy-start.1) | copy-done | bytes 1048600
  75.8 4.1 %shard_map.178 = (f32[8,512]{1,0:T(8,128)}, f32[8,512]{1,0:T(8,128)}) custom-call(s32[1]{0:T(128)} %bitcast.dir_ref, bf16[2,1024,256]{2,1,0:T(8,128)(2,1)} %bitcast.16, bf16[1024,1024]{1,0:T(8,128)(2,1)} %constant.50.clone.inv_ref, f32[1,1024]{1,0:T(1,128)} %constant_dynamic-slice_fusion.1.field_ref, f32[3,256]{1,0:T(4,128)} %constant_dynamic-slice_fusion.orient_ref, ...), custom_call_target="tpu_custom_call" | custom-call | tf_op jit(solution)/shard_map/pallas_call | solution.py:269
  79.9 0.3 collective-permute-start
  80.1 3.7 %collective-permute-done = f32[8,512]{1,0:T(8,128)S(1)} collective-permute-done((f32[8,512]{1,0:T(8,128)}, f32[8,512]{1,0:T(8,128)S(1)}, u32[]{:S(2)}, u32[]{:S(2)}) %collective-permute-start) | collective-permute-done | bytes 16416 | tf_op jit(solution)/shard_map/ppermute | solution.py:326
  83.8 0.7 add.18
  84.6 0.6 slice.8
  85.1 0.6 copy.21
  (2 shorter events, 0.0 us)
Async XLA Ops:
  0.6 24.4 %copy-start = (bf16[512,441]{0,1:T(8,128)(2,1)S(1)}, bf16[512,441]{0,1:T(8,128)(2,1)}, u32[]{:S(2)}) copy-start(bf16[512,441]{0,1:T(8,128)(2,1)} %param.22) | copy-start | bytes 1354756
  11.4 13.7 %copy-start.5 = (bf16[441,512]{1,0:T(8,128)(2,1)S(1)}, bf16[441,512]{1,0:T(8,128)(2,1)}, u32[]{:S(2)}) copy-start(bf16[441,512]{1,0:T(8,128)(2,1)} %param.21) | copy-start | bytes 1354756
  11.4 13.7 %copy-start.6 = (f32[441]{0:T(512)S(1)}, f32[441]{0:T(512)}, u32[]{:S(2)}) copy-start(f32[441]{0:T(512)} %param.23) | copy-start | bytes 5296
  11.4 29.7 %all-to-all-start = ((bf16[64,16,512]{2,1,0:T(8,128)(2,1)}), bf16[64,16,512]{2,1,0:T(8,128)(2,1)S(1)}, u32[]{:S(2)}, u32[]{:S(2)}) async-start(bf16[64,16,512]{2,1,0:T(8,128)(2,1)} %shard_map.176), calls=%async_computation | async-start | bytes 2097152 | tf_op jit(solution)/shard_map/all_to_all | solution.py:306
  41.1 1.0 %copy-start.2 = (bf16[64,16,512]{2,1,0:T(8,128)(2,1)}, bf16[64,16,512]{2,1,0:T(8,128)(2,1)S(1)}, u32[]{:S(2)}) copy-start(bf16[64,16,512]{2,1,0:T(8,128)(2,1)S(1)} %all-to-all-done.x_ref) | copy-start | bytes 3145732
  50.3 5.8 %copy-start.4 = (f32[512]{0:T(512)S(1)}, f32[512]{0:T(512)}, u32[]{:S(2)}) copy-start(f32[512]{0:T(512)} %param.20) | copy-start | bytes 6148
  50.3 6.4 %copy-start.3 = (f32[3,512]{1,0:T(4,128)S(1)}, f32[3,512]{1,0:T(4,128)}, u32[]{:S(2)}) copy-start(f32[3,512]{1,0:T(4,128)} %param.19) | copy-start | bytes 18436
  50.3 24.5 %all-to-all-start.1 = ((bf16[128,16,256]{2,1,0:T(8,128)(2,1)}), bf16[128,16,256]{2,1,0:T(8,128)(2,1)S(1)}, u32[]{:S(2)}, u32[]{:S(2)}) async-start(bf16[128,16,256]{2,1,0:T(8,128)(2,1)} %bitcast.17), calls=%async_computation.1 | async-start | bytes 2097152 | tf_op jit(solution)/shard_map/all_to_all | solution.py:314
  74.8 1.0 %copy-start.1 = (bf16[128,16,256]{2,1,0:T(8,128)(2,1)}, bf16[128,16,256]{2,1,0:T(8,128)(2,1)S(1)}, u32[]{:S(2)}) copy-start(bf16[128,16,256]{2,1,0:T(8,128)(2,1)S(1)} %all-to-all-done.1) | copy-start | bytes 3145732
  79.9 3.9 %collective-permute-start = (f32[8,512]{1,0:T(8,128)}, f32[8,512]{1,0:T(8,128)S(1)}, u32[]{:S(2)}, u32[]{:S(2)}) collective-permute-start(f32[8,512]{1,0:T(8,128)} %get-tuple-element.5), channel_id=1, source_target_pairs={{0,64},{64,0},{1,65},{65,1},{2,66},{66,2},{3,67},{67,3},{4,68},{68... | collective-permute-start | bytes 49160 | tf_op jit(solution)/shard_map/ppermute | solution.py:326
where the time goes:
time: 86.3 us; the launch traced here: 85.8 us
  waiting for transfers between devices  34.5 us (40%)
  Pallas kernels  21.5 us (25%)
  starting transfers between devices  17.6 us (20%)
  local copies, waits for them, and re-layouts  8.56 us (10%)
  other arithmetic  1.47 us (2%)
  matrix products  1.36 us (2%)
    pallas_call x3, Pallas kernels, call(): pl.pallas_call(kernel, out_shape=out_shape, in_specs=specs, out_specs=jax...  21.5 us
    all_to_all x1, waiting for transfers between devices, on_device(): lax.all_to_all(mixed.reshape(128, 16, 256), ('dir', 'shard'), split_axis=...  16.1 us
    all_to_all x1, waiting for transfers between devices, on_device(): lax.all_to_all(first, 'shard', split_axis=0, concat_axis=0, tiled=True)  14.7 us
    all_to_all x1, starting transfers between devices, on_device(): lax.all_to_all(first, 'shard', split_axis=0, concat_axis=0, tiled=True)  11.6 us
    all_to_all x1, starting transfers between devices, on_device(): lax.all_to_all(mixed.reshape(128, 16, 256), ('dir', 'shard'), split_axis=...  5.76 us
    ppermute x1, waiting for transfers between devices, on_device(): total = keep + lax.ppermute(send, 'dir', [(0, 1), (1, 0)])  3.7 us
    unnamed x16, local copies, waits for them, and re-layouts  3.5 us
  transfers between devices with their start and end apart: 3, of which 3 were waited for; matrix products, arithmetic and copies ran while one was open for 7% of the time, Pallas kernels for 0%

commit v1 on v0

v1 whole, which is shorter than its diff:
```python
import functools
import math

import jax
import jax.numpy as jnp
import numpy as np
from jax import lax
from jax.experimental import pallas as pl
from jax.experimental.pallas import tpu as pltpu
from jax.sharding import PartitionSpec as P

NX = 64
NY = 64
NZ = 16
M = 512
CELLS = NY * NZ
SHARDS = 64
LOCAL = M // SHARDS
TRANSPORT = 1.5
THIRD = 1.0 / 3.0
BF = jnp.bfloat16
F32 = jnp.float32


def slot_list():
    plain, nyquist = [], []
    for kz in range(1, 8):
        for ky in range(64):
            (nyquist if ky == 32 else plain).append(((ky, kz), (ky, kz), True))
    for ky in range(1, 32):
        plain.append(((ky, 0), (ky, 0), True))
        nyquist.append(((ky, 8), (ky, 8), True))
    nyquist.append(((0, 0), (0, 8), False))
    nyquist.append(((32, 0), (32, 8), False))
    return plain + nyquist


def point_waves(point):
    ky, kz = point
    fy = ky if ky <= 31 else ky - 64
    fz = kz if kz <= 7 else kz - 16
    rest = (0.0 if ky == 32 else fy / 64.0, 0.0 if kz == 8 else fz / 16.0)
    nyq = (-0.5 if ky == 32 else 0.0, -0.5 if kz == 8 else 0.0)
    return rest, nyq


@functools.lru_cache(maxsize=None)
def tables():
    slots = slot_list()
    y = np.arange(64)[:, None]
    z = np.arange(16)[None, :]
    forward = np.zeros((64, 2, 8, CELLS))
    weight = np.zeros((64, 2, 8))
    waves = np.zeros((8, 64, 2, 8), np.float32)
    for at, (re_point, im_point, paired) in enumerate(slots):
        group, slot = divmod(at, 8)
        for part, point in enumerate((re_point, im_point)):
            angle = 2.0 * math.pi * (((point[0] * y) % 64) / 64.0 + ((point[1] * z) % 16) / 16.0)
            row = -np.sin(angle) if (paired and part == 1) else np.cos(angle)
            forward[group, part, slot] = row.reshape(-1)
            weight[group, part, slot] = (2.0 if paired else 1.0) / CELLS
            rest, nyq = point_waves(point)
            waves[:5, group, part, slot] = rest + nyq + (weight[group, part, slot],)
    forward = forward.reshape(1024, CELLS)
    groups = np.zeros((64, 8, 128), np.float32)
    for group in range(64):
        for flag in range(2):
            groups[group, :4, flag * 16 : flag * 16 + 16] = waves[:4, group].reshape(4, 16)
            groups[group, 4, flag * 16 : flag * 16 + 16] = -0.5 * flag
            groups[group, 5, flag * 16 : flag * 16 + 16] = waves[4, group].reshape(16)
    x = np.arange(64)[:, None]
    j = np.arange(32)[None, :]
    angle = 2.0 * math.pi * ((x * j) % 64) / 64.0
    cosine = np.cos(angle)
    sine = -np.sin(angle)
    partner_c, partner_s = sine.copy(), -cosine
    sine[:, 0] = (-1.0) ** np.arange(64)
    partner_s[:, 0] = 0.0
    partner_c[:, 0] = 0.0
    fx = np.concatenate([cosine, sine], 1)
    fx_partner = np.concatenate([partner_c, partner_s], 1)
    wx = np.full(64, 2.0 / 64)
    wx[0] = wx[32] = 1.0 / 64
    fx_inv = (fx * wx[None, :]).T
    inv_x = np.zeros((64, 16, 16, 64))
    for r in range(16):
        inv_x[:, r, r, :] = fx_inv.T
    eye4 = np.eye(4)
    half = lambda v: v.astype(np.float32).astype(BF)
    return dict(
        forward=half(forward.reshape(64, 2, 8, CELLS).transpose(1, 0, 2, 3).reshape(1024, CELLS)),
        waves=waves.transpose(0, 2, 1, 3).reshape(8, 1024),
        groups=groups,
        fx=fx.astype(np.float32),
        fxp=fx_partner.astype(np.float32),
        fxi=half(np.tile(fx_inv.T, (4, 1))),
        inv_x=half(inv_x.reshape(1024, 1024)),
        fx4=half(np.kron(eye4, fx)),
        fxp4=half(np.kron(eye4, fx_partner)),
    )


def turns_cos(t):
    return turns_sin(t + 0.25)


def turns_sin(t):
    r = t - jnp.round(t)
    r = jnp.where(r > 0.25, 0.5 - r, jnp.where(r < -0.25, -0.5 - r, r))
    v = r * (2.0 * math.pi)
    s = v * v
    p = -2.5052108e-8
    p = p * s + 2.7557319e-6
    p = p * s - 1.9841270e-4
    p = p * s + 8.3333333e-3
    p = p * s - 1.6666667e-1
    return v + v * s * p


def dot(a, b):
    return jnp.dot(a, b, preferred_element_type=F32)


def dot_nt(a, b):
    return lax.dot_general(a, b, (((1,), (1,)), ((), ())), preferred_element_type=F32)


def split2(v):
    hi = v.astype(BF)
    lo = (v - hi.astype(F32)).astype(BF)
    return hi, lo


def direction_scale():
    return TRANSPORT * (1.0 - 2.0 * lax.axis_index("dir").astype(F32))


def step_one_kernel(
    orient_ref, waves_ref, fx_ref, fxp_ref, fxi_ref, q_hbm, fwd_hbm, field_hbm,
    out_hbm, q_ref, fwd_ref, field_ref, turned_ref, moved_ref, out_ref, sems,
):
    order = [pl.ds(at, 256) for at in (0, 512, 256, 768)]
    copies = [pltpu.make_async_copy(q_hbm, q_ref, sems.at[4])]
    copies += [pltpu.make_async_copy(fwd_hbm.at[at], fwd_ref.at[at], sems.at[i]) for i, at in enumerate(order)]
    copies += [pltpu.make_async_copy(field_hbm, field_ref, sems.at[5])]
    for copy in copies:
        copy.start()
    mine = lax.axis_index("shard") * LOCAL + lax.broadcasted_iota(jnp.int32, (8, 512), 0)
    chosen = (lax.broadcasted_iota(jnp.int32, (8, 512), 1) == mine).astype(F32) * direction_scale()
    hx, hy, hz = [jnp.sum(chosen * orient_ref[i : i + 1, :], 1, keepdims=True) for i in range(3)]
    w = waves_ref[...]
    rest = hy * w[0:1] + hz * w[1:2]
    nyq = hy * w[2:3] + hz * w[3:4]
    c, s = turns_cos(rest) * w[4:5], turns_sin(rest) * w[4:5]
    cn, sn = turns_cos(nyq), turns_sin(nyq) * turns_sin(hx * -0.5)
    plain = c * cn, (s * cn)[:, :512]
    tail = c * sn, (s * sn)[:, :512]
    lane_j = lax.broadcasted_iota(jnp.int32, (8, 64), 1)
    freq = (lane_j % 32).astype(F32) * (1.0 / 64.0)
    is_nyq = lane_j == 32
    cx = jnp.where(is_nyq, turns_cos(hx * -0.5), turns_cos(hx * freq))
    sx = jnp.where(is_nyq, 0.0, turns_sin(hx * freq))
    iota_r = lax.broadcasted_iota(jnp.int32, (256, 256), 0)
    iota_c = lax.broadcasted_iota(jnp.int32, (256, 256), 1)
    same = iota_r // 64 == iota_c // 64
    twice = jnp.concatenate([fxi_ref[...]] * 2, 1)
    shift_x = []
    for i in range(2):
        rows = [fx_ref[...] * cx[m : m + 1] + fxp_ref[...] * sx[m : m + 1] for m in range(4 * i, 4 * i + 4)]
        rows2 = jnp.concatenate(split2(jnp.concatenate(rows, 0)), 1)
        shift_x.append(jnp.where(same, dot_nt(twice, rows2), 0.0).astype(BF))
    nyq_x = jnp.where(same, jnp.where((iota_r + iota_c) % 2 == 1, 1.0 / 64, -1.0 / 64), 0.0).astype(BF)

    def rotate(re, im, table, at, width):
        out_re, out_im = [], []
        for m in range(LOCAL):
            rows = slice(m * 64, m * 64 + 64)
            a = table[0][m : m + 1, at : at + width]
            d = table[0][m : m + 1, 512 + at : 512 + at + width]
            b = table[1][m : m + 1, at : at + width]
            out_re.append((a * re[rows] + b * im[rows]).astype(BF))
            out_im.append((d * im[rows] - b * re[rows]).astype(BF))
        return jnp.concatenate(out_re, 0), jnp.concatenate(out_im, 0)

    copies[0].wait()
    for block in range(2):
        at = block * 256
        copies[1 + 2 * block].wait()
        copies[2 + 2 * block].wait()
        re = dot_nt(q_ref[...], fwd_ref[at : at + 256, :])
        im = dot_nt(q_ref[...], fwd_ref[512 + at : 768 + at, :])
        u = rotate(re, im, plain, at, 256)
        for part in range(2):
            for i in range(2):
                rows = slice(i * 256, i * 256 + 256)
                done = dot(shift_x[i], u[part][rows])
                lanes = part * 512 + at
                if block == 1:
                    if i == 0:
                        extra = rotate(re[:, 128:], im[:, 128:], tail, 384, 128)
                    turned_ref[rows, lanes : lanes + 128] = done[:, :128].astype(BF)
                    more = done[:, 128:] + dot(nyq_x, extra[part][rows])
                    turned_ref[rows, lanes + 128 : lanes + 256] = more.astype(BF)
                else:
                    turned_ref[rows, lanes : lanes + 256] = done.astype(BF)
    copies[5].wait()
    damp = jnp.exp(-field_ref[...])
    sends = []
    for i in range(2):
        rows = slice(i * 256, i * 256 + 256)
        moved = dot(turned_ref[rows, :], fwd_ref[...])
        for m in range(4):
            moved_ref[i * 256 + m * 64 : i * 256 + m * 64 + 64, :] = (moved[m * 64 : m * 64 + 64] * damp).astype(BF)
        out = dot_nt(fwd_ref[...], moved_ref[rows, :]).astype(BF)
        lanes = pl.ds(i * 256, 256)
        for part in range(2):
            out_ref[:, part * 8 : part * 8 + 8, lanes] = out[part * 512 : part * 512 + 512].reshape(64, 8, 256)
        sends.append(pltpu.make_async_copy(out_ref.at[:, :, lanes], out_hbm.at[:, :, lanes], sems.at[6 + i]))
        sends[i].start()
    for send in sends:
        send.wait()


def prepare_kernel(
    orient_ref, synthesis_ref, analysis_ref, decay_ref, groups_ref, fwd_ref,
    d_first_ref, d_ref, tc_ref, ts_ref, cx_ref, sx_ref, inv_ref,
):
    inv_ref[...] = fwd_ref[...].T
    scaled = (analysis_ref[...].astype(F32) * decay_ref[...]).astype(BF)
    d_ref[...] = dot(synthesis_ref[...], scaled).astype(BF)
    row = lax.broadcasted_iota(jnp.int32, (512, 512), 0)
    col = lax.broadcasted_iota(jnp.int32, (512, 512), 1)
    perm = ((row % 8) * 64 + row // 8 == col).astype(BF)
    d_first_ref[...] = dot(d_ref[...], perm).astype(BF)
    o = orient_ref[...] * direction_scale()
    head = jnp.concatenate([o, o, o[:2]], 0).T
    hx, hy, hz = head[:, 0:1], head[:, 1:2], head[:, 2:3]
    lane = lax.broadcasted_iota(jnp.int32, (512, 128), 1) % 64
    freq = (lane % 32).astype(F32) * (1.0 / 64.0)
    is_nyq = lane == 32
    cx_ref[...] = jnp.where(is_nyq, 1.0, turns_cos(hx * freq))
    sx_ref[...] = jnp.where(is_nyq, 0.0, turns_sin(hx * freq))
    w = groups_ref[lax.axis_index("shard")]
    rest = hy * w[0:1] + hz * w[1:2]
    cn = turns_cos(hx * w[4:5] + hy * w[2:3] + hz * w[3:4]) * w[5:6]
    tc_ref[...] = jnp.concatenate(split2(turns_cos(rest) * cn), 1)
    ts_ref[...] = jnp.concatenate(split2(turns_sin(rest) * cn), 1)


def mix_kernel(
    x_ref, d_first_ref, d_ref, tc_ref, ts_ref, cx_ref, sx_ref, fx_hbm, fxp_hbm, fxi_hbm, out_ref,
    wide_ref, mixed_ref, turned_ref, last_ref, fx_ref, fxp_ref, fxi_ref, sems,
):
    pairs = [(fx_hbm, fx_ref), (fxp_hbm, fxp_ref), (fxi_hbm, fxi_ref)]
    copies = [pltpu.make_async_copy(src, dst, sems.at[i]) for i, (src, dst) in enumerate(pairs)]
    for copy in copies:
        copy.start()
    left = lax.broadcasted_iota(jnp.int32, (64, 128), 1) < 64
    for quad in range(4):
        wide_ref[quad] = x_ref[:, :, quad * 128 : (quad + 1) * 128].reshape(1024, 128).astype(F32)
        for pair in range(8):
            first = wide_ref[quad, pl.ds(2 * pair, 64, stride=16), :]
            second = wide_ref[quad, pl.ds(2 * pair + 1, 64, stride=16), :]
            even = jnp.where(left, first, pltpu.roll(second, 64, 1))
            odd = jnp.where(left, pltpu.roll(first, 64, 1), second)
            mixed_ref[pl.ds(2 * quad * 64, 64), pl.ds(pair * 128, 128)] = even.astype(BF)
            mixed_ref[pl.ds((2 * quad + 1) * 64, 64), pl.ds(pair * 128, 128)] = odd.astype(BF)
    for copy in copies[:2]:
        copy.wait()
    src = lax.broadcasted_iota(jnp.int32, (256, 256), 0) % 128
    dst = lax.broadcasted_iota(jnp.int32, (256, 256), 1)
    cx = jnp.concatenate([cx_ref[...]] * 2, 1)
    sx = jnp.concatenate([sx_ref[...]] * 2, 1)

    def turn(at):
        piece = dot(d_first_ref[...], mixed_ref[:, at : at + 256]).astype(BF)
        return cx * dot(piece, fx_ref[...]) + sx * dot(piece, fxp_ref[...])

    for part in range(2):
        want = jnp.where(dst % 64 == 32, 16, 0) + dst // 64 + 4 * part
        pick_re = (src == want).astype(BF)
        pick_im = (src == want + 8).astype(BF)
        a = dot(tc_ref[...], pick_re)
        d = dot(tc_ref[...], pick_im)
        b = dot(ts_ref[...], pick_re)
        at = part * 256
        re, im = turn(at), turn(at + 512)
        turned_ref[:, at : at + 256] = (a * re + b * im).astype(BF)
        turned_ref[:, at + 512 : at + 768] = (d * im - b * re).astype(BF)
    for part in range(2):
        at = part * 256
        last_ref[at : at + 256, :] = dot(d_ref[at : at + 256, :], turned_ref[...]).astype(BF)
        if part == 0:
            copies[2].wait()
        out = dot_nt(fxi_ref[...], last_ref[at : at + 256, :]).astype(BF)
        out_ref[part] = out.reshape(64, 16, 256)


def moment_kernel(x_ref, orient_ref, weight_ref, inv_ref, field_hbm, keep_ref, send_ref, field_ref, sem):
    shard = lax.axis_index("shard")
    base = pl.multiple_of(shard // 8 * 8, 8)
    copy = pltpu.make_async_copy(field_hbm.at[pl.ds(base, 8)], field_ref, sem)
    copy.start()
    first_half = lax.axis_index("dir") == 0
    pick = lambda v: jnp.where(first_half, v[:, :256], v[:, 256:])
    o = pick(orient_ref[...])
    ux, uy, uz = o[0:1], o[1:2], o[2:3]
    rows = [jnp.ones_like(ux), ux * ux - THIRD, uy * uy - THIRD, ux * uy, ux * uz, uy * uz, 0.0 * ux, 0.0 * ux]
    g = jnp.concatenate(rows, 0) * pick(weight_ref[...])
    g = jnp.concatenate([g, jnp.zeros((120, 256), F32)], 0).T
    g_hi, g_lo = split2(g)
    parts = []
    x = x_ref[...].reshape(2, 64, 2, 8, 256)
    x = [jnp.concatenate([x[p, :, 0].reshape(512, 256), x[p, :, 1].reshape(512, 256)], 0) for p in range(2)]
    for block in range(4):
        inv = inv_ref[block * 256 : block * 256 + 256, :]
        hi, lo = split2(dot(inv, x[0]) * dot(inv, x[1]))
        parts.append((dot(hi, g_hi) + dot(lo, g_hi) + dot(hi, g_lo)).T[:8])
    result = jnp.concatenate(parts, 1)
    copy.wait()
    damp = jnp.exp(-field_ref[pl.ds(shard - base, 1), :])
    result = result * (damp * damp)
    keep_ref[...] = jnp.where(first_half, result[:, :512], result[:, 512:])
    send_ref[...] = jnp.where(first_half, result[:, 512:], result[:, :512])


def finish_kernel(keep_ref, got_ref, density_ref, tensor_ref):
    total = keep_ref[...] + got_ref[...]
    density_ref[...] = total[:1]
    for row in range(5):
        tensor_ref[row] = total[row + 1 : row + 2]


def on_chip(value):
    return pltpu.with_memory_space_constraint(value, pltpu.VMEM)


def call(kernel, out_shape, args, in_hbm=(), scratch=(), hbm_out=False):
    return pl.pallas_call(
        kernel,
        out_shape=out_shape,
        in_specs=[pl.BlockSpec(memory_space=pl.ANY if i in in_hbm else pltpu.VMEM) for i in range(len(args))],
        out_specs=jax.tree.map(lambda _: pl.BlockSpec(memory_space=pl.ANY if hbm_out else pltpu.VMEM), out_shape),
        scratch_shapes=list(scratch),
        compiler_params=pltpu.CompilerParams(vmem_limit_bytes=56 * 1024 * 1024),
    )(*args)


def on_device(propagators, field, orient, quad_weights, analysis, synthesis, decay):
    tab = {name: jnp.asarray(value) for name, value in tables().items()}
    sds, vm = jax.ShapeDtypeStruct, pltpu.VMEM
    state = propagators.reshape(LOCAL * NX, CELLS)
    first = call(
        step_one_kernel,
        sds((64, 16, 512), BF),
        (orient, tab["waves"], tab["fx"], tab["fxp"], tab["fxi"], state, tab["forward"], field),
        (5, 6, 7),
        (vm((512, 1024), BF), vm((1024, 1024), BF), vm((64, 1024), F32), vm((512, 1024), BF), vm((512, 1024), BF),
         vm((64, 16, 512), BF), pltpu.SemaphoreType.DMA((8,))),
        hbm_out=True,
    )
    gathered = lax.all_to_all(first, "shard", split_axis=0, concat_axis=0, tiled=True)
    *prepared, inverse = call(
        prepare_kernel,
        (vm((512, 512), BF), vm((512, 512), BF), vm((512, 256), BF), vm((512, 256), BF),
         vm((512, 128), F32), vm((512, 128), F32), sds((1024, 1024), BF)),
        (orient, synthesis, analysis, decay[:, None], tab["groups"], tab["forward"]),
    )
    mixed = call(
        mix_kernel,
        vm((2, 64, 16, 256), BF),
        tuple(on_chip(v) for v in (gathered, *prepared)) + (tab["fx4"], tab["fxp4"], tab["inv_x"]),
        (7, 8, 9),
        (vm((4, 1024, 128), F32), vm((512, 1024), BF), vm((512, 1024), BF), vm((512, 1024), BF), vm((256, 256), BF),
         vm((256, 256), BF), vm((1024, 1024), BF), pltpu.SemaphoreType.DMA((3,))),
    )
    planes = lax.all_to_all(
        mixed.reshape(128, 16, 256), ("dir", "shard"), split_axis=0, concat_axis=0, tiled=True
    ).reshape(2, 1024, 256)
    keep, send = call(
        moment_kernel,
        (vm((8, 512), F32), vm((8, 512), F32)),
        (on_chip(planes), orient, quad_weights[None], on_chip(inverse), field),
        (4,),
        (vm((8, 1024), F32), pltpu.SemaphoreType.DMA),
    )
    got = lax.ppermute(send, "dir", [(0, 1), (1, 0)])
    density, tensor = call(finish_kernel, (sds((1, 512), F32), sds((5, 1, 512), F32)), (on_chip(keep), on_chip(got)))
    return density, tensor


def solution(mesh):
    in_specs = (P("dir", "shard", None, None), P(), P(), P(), P(), P(), P())
    out_specs = (P("shard", "dir"), P(None, "shard", "dir"))
    return jax.shard_map(on_device, mesh=mesh, in_specs=in_specs, out_specs=out_specs, check_vma=False)
```

time: 86.3 us -> 77 us (0.89)
  blocking collectives: 0 us -> 24.3 us
  waiting for transfers between devices: 34.5 us -> 14.2 us
  local copies, waits for them, and re-layouts: 8.56 us -> 1.83 us
  starting transfers between devices: 17.6 us -> 12.1 us
  Pallas kernels: 21.5 us -> 23.4 us
  other arithmetic: 1.47 us -> 0 us
  matrix products: 1.36 us -> 0 us
    all_to_all x0 -> x1, blocking collectives: none -> 24.3 us  [on_device(): lax.all_to_all(mixed.reshape(128, 16, 256), ('dir', 'shard'), split_axis=...]
    all_to_all x1 -> x0, waiting for transfers between devices: 16.1 us -> none  [on_device(): lax.all_to_all(mixed.reshape(128, 16, 256), ('dir', 'shard'), split_axis=...]
    all_to_all x1 -> x0, starting transfers between devices: 5.76 us -> none  [on_device(): lax.all_to_all(mixed.reshape(128, 16, 256), ('dir', 'shard'), split_axis=...]
    all_to_all x1, waiting for transfers between devices: 14.7 us -> 10.7 us  [on_device(): lax.all_to_all(first, 'shard', split_axis=0, concat_axis=0, tiled=True)]
    dynamic_slice x4 -> x0, local copies, waits for them, and re-layouts: 3.19 us -> none  [the longest x1 1.36 us: on_device(): local_field = lax.dynamic_slice_in_dim(field, shard, 1, 0)]
    unnamed x16 -> x7, local copies, waits for them, and re-layouts: 3.5 us -> 1.01 us
    pallas_call x3 -> x5, Pallas kernels: 21.5 us -> 23.4 us  [call(): pl.pallas_call(kernel, out_shape=out_shape, in_specs=[pl.BlockSpec(memory...]
    dot_general x1 -> x0, matrix products: 1.36 us -> none  [on_device(): jnp.dot(synthesis, (analysis.astype(F32) * decay[:, None]).astype(BF), pr...]
  transfers between devices with their start and end apart: 3 -> 2, of which waited for: 3 -> 2; matrix products, arithmetic and copies ran while one was open for 7% -> 2% of each run, Pallas kernels for 0% -> 7%
where the time goes in v1:
time: 77 us; the launch traced here: 76.6 us
  blocking collectives  24.3 us (32%)
  Pallas kernels  23.4 us (30%)
  waiting for transfers between devices  14.2 us (18%)
  starting transfers between devices  12.1 us (16%)
  local copies, waits for them, and re-layouts  1.83 us (2%)
    all_to_all x1, blocking collectives, on_device(): lax.all_to_all(mixed.reshape(128, 16, 256), ('dir', 'shard'), split_axis=...  24.3 us
    pallas_call x5, Pallas kernels, call(): pl.pallas_call(kernel, out_shape=out_shape, in_specs=[pl.BlockSpec(memory...  23.4 us
    all_to_all x1, starting transfers between devices, on_device(): lax.all_to_all(first, 'shard', split_axis=0, concat_axis=0, tiled=True)  11.8 us
    all_to_all x1, waiting for transfers between devices, on_device(): lax.all_to_all(first, 'shard', split_axis=0, concat_axis=0, tiled=True)  10.7 us
    ppermute x1, waiting for transfers between devices, on_device(): got = lax.ppermute(send, 'dir', [(0, 1), (1, 0)])  3.5 us
  transfers between devices with their start and end apart: 2, of which 2 were waited for; matrix products, arithmetic and copies ran while one was open for 2% of the time, Pallas kernels for 7%

profile of v1, /device:TPU:0, one launch (start us, length us, event | category | flops | bytes accessed | tf_op | source)
XLA Modules:
  0.0 76.6 jit_solution(1622721055708960365)
XLA Ops:
  0.6 8.2 %shard_map.167 = bf16[64,16,512]{2,1,0:T(8,128)(2,1)} custom-call(f32[3,512]{1,0:T(4,128)} %orient_ref.5, f32[8,1024]{1,0:T(8,128)} %constant.19.clone.waves_ref, f32[64,64]{1,0:T(8,128)} %constant.21.clone.fx_ref, f32[64,64]{1,0:T(8,128)} %constant.22.clone.fxp_ref, bf16[256,64]{1,0:T(8,128)(2,1)} %constant.23.clone.fxi_ref, bf16[512,1024]{1,0:T(8,128)(2,1)} %bitcast.7, ...), custom_call_target="tpu_custom_call" | custom-call | tf_op jit(solution)/shard_map/pallas_call | solution.py:339
  8.9 0.0 copy-start.2
  8.9 0.0 copy-start.1
  8.9 11.8 %all-to-all-start = ((bf16[64,16,512]{2,1,0:T(8,128)(2,1)}), bf16[64,16,512]{2,1,0:T(8,128)(2,1)S(1)}, u32[]{:S(2)}, u32[]{:S(2)}) async-start(bf16[64,16,512]{2,1,0:T(8,128)(2,1)} %shard_map.167), calls=%async_computation | async-start | bytes 2097152 | tf_op jit(solution)/shard_map/all_to_all | solution.py:362
  20.7 0.0 copy-done.2
  20.7 0.8 %copy.20.decay_ref = f32[441,1]{1,0:T(8,128)} copy(f32[441,1]{0,1:T(1,128)S(1)} %bitcast.8) | data formatting | bytes 3528 | tf_op jit(solution)/shard_map/broadcast_in_dim | solution.py:367
  21.6 0.0 copy-done.1
  21.6 1.0 %copy.19.synthesis_ref = bf16[512,441]{1,0:T(8,128)(2,1)} copy(bf16[512,441]{0,1:T(8,128)(2,1)S(1)} %copy-done.1) | data formatting | bytes 903168 | tf_op args[5]
  22.6 5.4 %shard_map.168 = (bf16[512,512]{1,0:T(8,128)(2,1)S(1)}, bf16[512,512]{1,0:T(8,128)(2,1)S(1)}, bf16[512,256]{1,0:T(8,128)(2,1)S(1)}, bf16[512,256]{1,0:T(8,128)(2...) custom-call(f32[3,512]{1,0:T(4,128)} %orient_ref.5, ...), custom_call_target="tpu_custom_call" | custom-call | tf_op jit(solution)/shard_map/pallas_call | solution.py:339
  27.9 10.7 %all-to-all-done.x_ref = bf16[64,16,512]{2,1,0:T(8,128)(2,1)S(1)} async-done(((bf16[64,16,512]{2,1,0:T(8,128)(2,1)}), bf16[64,16,512]{2,1,0:T(8,128)(2,1)S(1)}, u32[]{:S(2)}, u32[]{:S(2)}) %all-to-all-start) | async-done | bytes 1048608 | tf_op jit(solution)/shard_map/all_to_all | solution.py:362
  38.6 6.0 %shard_map.169 = bf16[2,64,16,256]{3,2,1,0:T(8,128)(2,1)S(1)} custom-call(bf16[64,16,512]{2,1,0:T(8,128)(2,1)S(1)} %all-to-all-done.x_ref, bf16[512,512]{1,0:T(8,128)(2,1)S(1)} %get-tuple-element.11.d_first_ref, bf16[512,512]{1,0:T(8,128)(2,1)S(1)} %get-tuple-element.12.d_ref, bf16[512,256]{1,0:T(8,128)(2,1)S(1)} %get-tuple-element.13.tc_ref, ...), custom_call_target="tpu_custom_call" | custom-call | tf_op jit(solution)/shard_map/pallas_call | solution.py:339
  44.6 0.0 copy-start
  44.6 24.3 %all_to_all.10 = bf16[128,16,256]{2,1,0:T(8,128)(2,1)S(1)} all-to-all(bf16[128,16,256]{2,1,0:T(8,128)(2,1)S(1)} %bitcast.5), channel_id=1, replica_groups=mesh['dir'=2,'shard'=64] {'dir','shard'}, dimensions={0} | all-to-all | bytes 2097152 | tf_op jit(solution)/shard_map/all_to_all | solution.py:377
  68.9 0.0 copy-done
  68.9 3.2 %shard_map.170 = (f32[8,512]{1,0:T(8,128)S(1)}, f32[8,512]{1,0:T(8,128)S(1)}) custom-call(bf16[2,1024,256]{2,1,0:T(8,128)(2,1)S(1)} %bitcast.6, f32[3,512]{1,0:T(4,128)} %orient_ref.5, f32[1,512]{1,0:T(1,128)} %bitcast.9, bf16[1024,1024]{1,0:T(8,128)(2,1)S(1)} %copy-done, f32[64,1024]{1,0:T(8,128)} %field_hbm.3), custom_call_target="tpu_custom_call" | custom-call | tf_op jit(solution)/shard_map/pallas_call | solution.py:339
  72.1 0.3 collective-permute-start
  72.4 3.5 %collective-permute-done.got_ref = f32[8,512]{1,0:T(8,128)S(1)} collective-permute-done((f32[8,512]{1,0:T(8,128)S(1)}, f32[8,512]{1,0:T(8,128)S(1)}, u32[]{:S(2)}, u32[]{:S(2)}) %collective-permute-start) | collective-permute-done | bytes 16416 | tf_op jit(solution)/shard_map/ppermute | solution.py:387
  75.9 0.6 shard_map.171
Async XLA Ops:
  8.9 11.9 %copy-start.2 = (f32[441]{0:T(512)S(1)}, f32[441]{0:T(512)}, u32[]{:S(2)}) copy-start(f32[441]{0:T(512)} %param.22) | copy-start | bytes 5296
  8.9 12.7 %copy-start.1 = (bf16[512,441]{0,1:T(8,128)(2,1)S(1)}, bf16[512,441]{0,1:T(8,128)(2,1)}, u32[]{:S(2)}) copy-start(bf16[512,441]{0,1:T(8,128)(2,1)} %param.21) | copy-start | bytes 1354756
  8.9 29.7 %all-to-all-start = ((bf16[64,16,512]{2,1,0:T(8,128)(2,1)}), bf16[64,16,512]{2,1,0:T(8,128)(2,1)S(1)}, u32[]{:S(2)}, u32[]{:S(2)}) async-start(bf16[64,16,512]{2,1,0:T(8,128)(2,1)} %shard_map.167), calls=%async_computation | async-start | bytes 2097152 | tf_op jit(solution)/shard_map/all_to_all | solution.py:362
  44.6 24.3 %copy-start = (bf16[1024,1024]{1,0:T(8,128)(2,1)S(1)}, bf16[1024,1024]{1,0:T(8,128)(2,1)}, u32[]{:S(2)}) copy-start(bf16[1024,1024]{1,0:T(8,128)(2,1)} %get-tuple-element.17.inv_ref) | copy-start | bytes 6291460
  72.1 3.8 %collective-permute-start = (f32[8,512]{1,0:T(8,128)S(1)}, f32[8,512]{1,0:T(8,128)S(1)}, u32[]{:S(2)}, u32[]{:S(2)}) collective-permute-start(f32[8,512]{1,0:T(8,128)S(1)} %get-tuple-element.19), channel_id=1, source_target_pairs={{0,64},{64,0},{1,65},{65,1},{2,66},{66,2},{3,67},{67,3},{4,68},{68... | collective-permute-start | bytes 49160 | tf_op jit(solution)/shard_map/ppermute | solution.py:387

commit v2 on v1

--- a/solution.py
+++ b/solution.py
@@ -95,8 +95,7 @@
         fxp=fx_partner.astype(np.float32),
         fxi=half(np.tile(fx_inv.T, (4, 1))),
         inv_x=half(inv_x.reshape(1024, 1024)),
-        fx4=half(np.kron(eye4, fx)),
-        fxp4=half(np.kron(eye4, fx_partner)),
+        fx8=half(np.concatenate([np.kron(eye4, fx), np.kron(eye4, fx_partner)], 1)),
     )
 
 
@@ -143,7 +142,7 @@
     copies = [pltpu.make_async_copy(q_hbm, q_ref, sems.at[4])]
     copies += [pltpu.make_async_copy(fwd_hbm.at[at], fwd_ref.at[at], sems.at[i]) for i, at in enumerate(order)]
     copies += [pltpu.make_async_copy(field_hbm, field_ref, sems.at[5])]
-    for copy in copies:
+    for copy in copies[:3]:
         copy.start()
     mine = lax.axis_index("shard") * LOCAL + lax.broadcasted_iota(jnp.int32, (8, 512), 0)
     chosen = (lax.broadcasted_iota(jnp.int32, (8, 512), 1) == mine).astype(F32) * direction_scale()
@@ -187,6 +186,9 @@
         at = block * 256
         copies[1 + 2 * block].wait()
         copies[2 + 2 * block].wait()
+        if block == 0:
+            for copy in copies[3:]:
+                copy.start()
         re = dot_nt(q_ref[...], fwd_ref[at : at + 256, :])
         im = dot_nt(q_ref[...], fwd_ref[512 + at : 768 + at, :])
         u = rotate(re, im, plain, at, 256)
@@ -211,20 +213,33 @@
         moved = dot(turned_ref[rows, :], fwd_ref[...])
         for m in range(4):
             moved_ref[i * 256 + m * 64 : i * 256 + m * 64 + 64, :] = (moved[m * 64 : m * 64 + 64] * damp).astype(BF)
-        out = dot_nt(fwd_ref[...], moved_ref[rows, :]).astype(BF)
         lanes = pl.ds(i * 256, 256)
         for part in range(2):
-            out_ref[:, part * 8 : part * 8 + 8, lanes] = out[part * 512 : part * 512 + 512].reshape(64, 8, 256)
-        sends.append(pltpu.make_async_copy(out_ref.at[:, :, lanes], out_hbm.at[:, :, lanes], sems.at[6 + i]))
-        sends[i].start()
+            out = dot_nt(fwd_ref[part * 512 : part * 512 + 512, :], moved_ref[rows, :]).astype(BF)
+            at = (slice(None), pl.ds(part * 8, 8), lanes)
+            out_ref[at] = out.reshape(64, 8, 256)
+            send = pltpu.make_async_copy(out_ref.at[at], out_hbm.at[at], sems.at[6 + 2 * i + part])
+            send.start()
+            sends.append(send)
     for send in sends:
         send.wait()
 
 
 def prepare_kernel(
-    orient_ref, synthesis_ref, analysis_ref, decay_ref, groups_ref, fwd_ref,
-    d_first_ref, d_ref, tc_ref, ts_ref, cx_ref, sx_ref, inv_ref,
+    orient_ref, synthesis_ref, analysis_ref, decay_ref, groups_ref, fwd_ref, weight_ref, field_ref,
+    d_first_ref, d_ref, tc_ref, ts_ref, cx_ref, sx_ref, inv_ref, g_ref, damp_ref,
 ):
+    first_half = lax.axis_index("dir") == 0
+    pick = lambda v: jnp.where(first_half, v[:, :256], v[:, 256:])
+    u = pick(orient_ref[...])
+    ux, uy, uz = u[0:1], u[1:2], u[2:3]
+    rows = [jnp.ones_like(ux), ux * ux - THIRD, uy * uy - THIRD, ux * uy, ux * uz, uy * uz, 0.0 * ux, 0.0 * ux]
+    g = jnp.concatenate(rows, 0) * pick(weight_ref[...])
+    g = jnp.concatenate([g, jnp.zeros((120, 256), F32)], 0).T
+    g_hi, g_lo = split2(g)
+    g_ref[...] = jnp.concatenate([g_hi, g_hi, g_lo], 0)
+    damp = jnp.exp(-field_ref[pl.ds(lax.axis_index("shard"), 1), :])
+    damp_ref[...] = damp * damp
     inv_ref[...] = fwd_ref[...].T
     scaled = (analysis_ref[...].astype(F32) * decay_ref[...]).astype(BF)
     d_ref[...] = dot(synthesis_ref[...], scaled).astype(BF)
@@ -248,25 +263,30 @@
 
 
 def mix_kernel(
-    x_ref, d_first_ref, d_ref, tc_ref, ts_ref, cx_ref, sx_ref, fx_hbm, fxp_hbm, fxi_hbm, out_ref,
-    wide_ref, mixed_ref, turned_ref, last_ref, fx_ref, fxp_ref, fxi_ref, sems,
+    x_ref, d_first_ref, d_ref, tc_ref, ts_ref, cx_ref, sx_ref, fx_hbm, fxi_hbm, out_ref,
+    wide_ref, mixed_ref, turned_ref, last_ref, fx_ref, fxi_ref, sems,
 ):
-    pairs = [(fx_hbm, fx_ref), (fxp_hbm, fxp_ref), (fxi_hbm, fxi_ref)]
+    pairs = [(fx_hbm, fx_ref), (fxi_hbm, fxi_ref)]
     copies = [pltpu.make_async_copy(src, dst, sems.at[i]) for i, (src, dst) in enumerate(pairs)]
     for copy in copies:
         copy.start()
     left = lax.broadcasted_iota(jnp.int32, (64, 128), 1) < 64
     for quad in range(4):
         wide_ref[quad] = x_ref[:, :, quad * 128 : (quad + 1) * 128].reshape(1024, 128).astype(F32)
-        for pair in range(8):
-            first = wide_ref[quad, pl.ds(2 * pair, 64, stride=16), :]
-            second = wide_ref[quad, pl.ds(2 * pair + 1, 64, stride=16), :]
-            even = jnp.where(left, first, pltpu.roll(second, 64, 1))
-            odd = jnp.where(left, pltpu.roll(first, 64, 1), second)
-            mixed_ref[pl.ds(2 * quad * 64, 64), pl.ds(pair * 128, 128)] = even.astype(BF)
-            mixed_ref[pl.ds((2 * quad + 1) * 64, 64), pl.ds(pair * 128, 128)] = odd.astype(BF)
-    for copy in copies[:2]:
-        copy.wait()
+
+    def arrange(block):
+        for pair in (2 * block, 2 * block + 1):
+            for quad in range(4):
+                first = wide_ref[quad, pl.ds(2 * pair, 64, stride=16), :]
+                second = wide_ref[quad, pl.ds(2 * pair + 1, 64, stride=16), :]
+                even = jnp.where(left, first, pltpu.roll(second, 64, 1))
+                odd = jnp.where(left, pltpu.roll(first, 64, 1), second)
+                mixed_ref[pl.ds(2 * quad * 64, 64), pl.ds(pair * 128, 128)] = even.astype(BF)
+                mixed_ref[pl.ds((2 * quad + 1) * 64, 64), pl.ds(pair * 128, 128)] = odd.astype(BF)
+
+    arrange(0)
+    arrange(2)
+    copies[0].wait()
     src = lax.broadcasted_iota(jnp.int32, (256, 256), 0) % 128
     dst = lax.broadcasted_iota(jnp.int32, (256, 256), 1)
     cx = jnp.concatenate([cx_ref[...]] * 2, 1)
@@ -274,7 +294,8 @@
 
     def turn(at):
         piece = dot(d_first_ref[...], mixed_ref[:, at : at + 256]).astype(BF)
-        return cx * dot(piece, fx_ref[...]) + sx * dot(piece, fxp_ref[...])
+        both = dot(piece, fx_ref[...])
+        return cx * both[:, :256] + sx * both[:, 256:]
 
     for part in range(2):
         want = jnp.where(dst % 64 == 32, 16, 0) + dst // 64 + 4 * part
@@ -284,6 +305,9 @@
         d = dot(tc_ref[...], pick_im)
         b = dot(ts_ref[...], pick_re)
         at = part * 256
+        if part == 1:
+            arrange(1)
+            arrange(3)
         re, im = turn(at), turn(at + 512)
         turned_ref[:, at : at + 256] = (a * re + b * im).astype(BF)
         turned_ref[:, at + 512 : at + 768] = (d * im - b * re).astype(BF)
@@ -291,37 +315,22 @@
         at = part * 256
         last_ref[at : at + 256, :] = dot(d_ref[at : at + 256, :], turned_ref[...]).astype(BF)
         if part == 0:
-            copies[2].wait()
+            copies[1].wait()
         out = dot_nt(fxi_ref[...], last_ref[at : at + 256, :]).astype(BF)
         out_ref[part] = out.reshape(64, 16, 256)
 
 
-def moment_kernel(x_ref, orient_ref, weight_ref, inv_ref, field_hbm, keep_ref, send_ref, field_ref, sem):
-    shard = lax.axis_index("shard")
-    base = pl.multiple_of(shard // 8 * 8, 8)
-    copy = pltpu.make_async_copy(field_hbm.at[pl.ds(base, 8)], field_ref, sem)
-    copy.start()
-    first_half = lax.axis_index("dir") == 0
-    pick = lambda v: jnp.where(first_half, v[:, :256], v[:, 256:])
-    o = pick(orient_ref[...])
-    ux, uy, uz = o[0:1], o[1:2], o[2:3]
-    rows = [jnp.ones_like(ux), ux * ux - THIRD, uy * uy - THIRD, ux * uy, ux * uz, uy * uz, 0.0 * ux, 0.0 * ux]
-    g = jnp.concatenate(rows, 0) * pick(weight_ref[...])
-    g = jnp.concatenate([g, jnp.zeros((120, 256), F32)], 0).T
-    g_hi, g_lo = split2(g)
-    parts = []
+def moment_kernel(own, x_ref, g_ref, damp_ref, inv_ref, out_ref):
+    me = lax.axis_index("dir")
+    base = pl.multiple_of((me if own else 1 - me) * 512, 512)
     x = x_ref[...].reshape(2, 64, 2, 8, 256)
     x = [jnp.concatenate([x[p, :, 0].reshape(512, 256), x[p, :, 1].reshape(512, 256)], 0) for p in range(2)]
-    for block in range(4):
-        inv = inv_ref[block * 256 : block * 256 + 256, :]
+    parts = []
+    for block in range(2):
+        inv = inv_ref[pl.ds(base + block * 256, 256), :]
         hi, lo = split2(dot(inv, x[0]) * dot(inv, x[1]))
-        parts.append((dot(hi, g_hi) + dot(lo, g_hi) + dot(hi, g_lo)).T[:8])
-    result = jnp.concatenate(parts, 1)
-    copy.wait()
-    damp = jnp.exp(-field_ref[pl.ds(shard - base, 1), :])
-    result = result * (damp * damp)
-    keep_ref[...] = jnp.where(first_half, result[:, :512], result[:, 512:])
-    send_ref[...] = jnp.where(first_half, result[:, 512:], result[:, :512])
+        parts.append(dot(jnp.concatenate([hi, lo, hi], 1), g_ref[...]).T[:8])
+    out_ref[...] = jnp.concatenate(parts, 1) * damp_ref[:, pl.ds(base, 512)]
 
 
 def finish_kernel(keep_ref, got_ref, density_ref, tensor_ref):
@@ -356,35 +365,32 @@
         (orient, tab["waves"], tab["fx"], tab["fxp"], tab["fxi"], state, tab["forward"], field),
         (5, 6, 7),
         (vm((512, 1024), BF), vm((1024, 1024), BF), vm((64, 1024), F32), vm((512, 1024), BF), vm((512, 1024), BF),
-         vm((64, 16, 512), BF), pltpu.SemaphoreType.DMA((8,))),
+         vm((64, 16, 512), BF), pltpu.SemaphoreType.DMA((10,))),
         hbm_out=True,
     )
     gathered = lax.all_to_all(first, "shard", split_axis=0, concat_axis=0, tiled=True)
-    *prepared, inverse = call(
+    *prepared, inverse, g, damp = call(
         prepare_kernel,
         (vm((512, 512), BF), vm((512, 512), BF), vm((512, 256), BF), vm((512, 256), BF),
-         vm((512, 128), F32), vm((512, 128), F32), sds((1024, 1024), BF)),
-        (orient, synthesis, analysis, decay[:, None], tab["groups"], tab["forward"]),
+         vm((512, 128), F32), vm((512, 128), F32), sds((1024, 1024), BF),
+         sds((768, 128), BF), sds((1, 1024), F32)),
+        (orient, synthesis, analysis, decay[:, None], tab["groups"], tab["forward"], quad_weights[None], field),
     )
     mixed = call(
         mix_kernel,
         vm((2, 64, 16, 256), BF),
-        tuple(on_chip(v) for v in (gathered, *prepared)) + (tab["fx4"], tab["fxp4"], tab["inv_x"]),
-        (7, 8, 9),
-        (vm((4, 1024, 128), F32), vm((512, 1024), BF), vm((512, 1024), BF), vm((512, 1024), BF), vm((256, 256), BF),
-         vm((256, 256), BF), vm((1024, 1024), BF), pltpu.SemaphoreType.DMA((3,))),
+        tuple(on_chip(v) for v in (gathered, *prepared)) + (tab["fx8"], tab["inv_x"]),
+        (7, 8),
+        (vm((4, 1024, 128), F32), vm((512, 1024), BF), vm((512, 1024), BF), vm((512, 1024), BF), vm((256, 512), BF),
+         vm((1024, 1024), BF), pltpu.SemaphoreType.DMA((2,))),
     )
     planes = lax.all_to_all(
         mixed.reshape(128, 16, 256), ("dir", "shard"), split_axis=0, concat_axis=0, tiled=True
     ).reshape(2, 1024, 256)
-    keep, send = call(
-        moment_kernel,
-        (vm((8, 512), F32), vm((8, 512), F32)),
-        (on_chip(planes), orient, quad_weights[None], on_chip(inverse), field),
-        (4,),
-        (vm((8, 1024), F32), pltpu.SemaphoreType.DMA),
-    )
+    operands = tuple(on_chip(v) for v in (planes, g, damp, inverse))
+    send = call(functools.partial(moment_kernel, False), vm((8, 512), F32), operands)
     got = lax.ppermute(send, "dir", [(0, 1), (1, 0)])
+    keep = call(functools.partial(moment_kernel, True), vm((8, 512), F32), operands)
     density, tensor = call(finish_kernel, (sds((1, 512), F32), sds((5, 1, 512), F32)), (on_chip(keep), on_chip(got)))
     return density, tensor
 

time: 77 us -> 74.4 us (0.966)
  Pallas kernels: 23.4 us -> 21.6 us
    pallas_call x5 -> x6, Pallas kernels: 23.4 us -> 21.6 us  [call(): pl.pallas_call(kernel, out_shape=out_shape, in_specs=[pl.BlockSpec(memory...]
    ppermute x1, waiting for transfers between devices: 3.5 us -> 2.27 us  [on_device(): got = lax.ppermute(send, 'dir', [(0, 1), (1, 0)])]
  transfers between devices with their start and end apart: 2 -> 2, of which waited for: 2 -> 2; matrix products, arithmetic and copies ran while one was open for 2% -> 2% of each run, Pallas kernels for 7% -> 8%
where the time goes in v2:
time: 74.4 us; the launch traced here: 74.1 us
  blocking collectives  24.3 us (33%)
  Pallas kernels  21.6 us (29%)
  waiting for transfers between devices  13.6 us (18%)
  starting transfers between devices  12 us (16%)
  local copies, waits for them, and re-layouts  1.86 us (2%)
    all_to_all x1, blocking collectives, on_device(): lax.all_to_all(mixed.reshape(128, 16, 256), ('dir', 'shard'), split_axis=...  24.3 us
    pallas_call x6, Pallas kernels, call(): pl.pallas_call(kernel, out_shape=out_shape, in_specs=[pl.BlockSpec(memory...  21.6 us
    all_to_all x1, starting transfers between devices, on_device(): lax.all_to_all(first, 'shard', split_axis=0, concat_axis=0, tiled=True)  11.6 us
    all_to_all x1, waiting for transfers between devices, on_device(): lax.all_to_all(first, 'shard', split_axis=0, concat_axis=0, tiled=True)  11.3 us
    ppermute x1, waiting for transfers between devices, on_device(): got = lax.ppermute(send, 'dir', [(0, 1), (1, 0)])  2.27 us
  transfers between devices with their start and end apart: 2, of which 2 were waited for; matrix products, arithmetic and copies ran while one was open for 2% of the time, Pallas kernels for 8%

profile of v2, /device:TPU:0, one launch (start us, length us, event | category | flops | bytes accessed | tf_op | source)
XLA Modules:
  0.0 74.1 jit_solution(16797956177507838508)
XLA Ops:
  0.6 8.1 %shard_map.158 = bf16[64,16,512]{2,1,0:T(8,128)(2,1)} custom-call(f32[3,512]{1,0:T(4,128)} %orient_ref.3, f32[8,1024]{1,0:T(8,128)} %constant.17.clone.waves_ref, f32[64,64]{1,0:T(8,128)} %constant.19.clone.fx_ref, f32[64,64]{1,0:T(8,128)} %constant.20.clone.fxp_ref, bf16[256,64]{1,0:T(8,128)(2,1)} %constant.21.clone.fxi_ref, bf16[512,1024]{1,0:T(8,128)(2,1)} %bitcast.8, ...), custom_call_target="tpu_custom_call" | custom-call | tf_op jit(solution)/shard_map/pallas_call | solution.py:348
  8.7 0.0 copy-start.4
  8.7 0.0 copy-start.3
  8.8 11.6 %all-to-all-start = ((bf16[64,16,512]{2,1,0:T(8,128)(2,1)}), bf16[64,16,512]{2,1,0:T(8,128)(2,1)S(1)}, u32[]{:S(2)}, u32[]{:S(2)}) async-start(bf16[64,16,512]{2,1,0:T(8,128)(2,1)} %shard_map.158), calls=%async_computation | async-start | bytes 2097152 | tf_op jit(solution)/shard_map/all_to_all | solution.py:371
  20.4 0.0 copy-done.4
  20.4 0.8 %copy.19.decay_ref = f32[441,1]{1,0:T(8,128)} copy(f32[441,1]{0,1:T(1,128)S(1)} %bitcast.10) | data formatting | bytes 3528 | tf_op jit(solution)/shard_map/broadcast_in_dim | solution.py:377
  21.2 0.0 copy-done.3
  21.2 1.0 %copy.18.synthesis_ref = bf16[512,441]{1,0:T(8,128)(2,1)} copy(bf16[512,441]{0,1:T(8,128)(2,1)S(1)} %copy-done.3) | data formatting | bytes 903168 | tf_op args[5]
  22.3 4.9 %shard_map.159 = (bf16[512,512]{1,0:T(8,128)(2,1)S(1)}, bf16[512,512]{1,0:T(8,128)(2,1)S(1)}, bf16[512,256]{1,0:T(8,128)(2,1)S(1)}, bf16[512,256]{1,0:T(8,128)(2...) custom-call(f32[3,512]{1,0:T(4,128)} %orient_ref.3, ...), custom_call_target="tpu_custom_call" | custom-call | tf_op jit(solution)/shard_map/pallas_call | solution.py:348
  27.1 11.3 %all-to-all-done.x_ref = bf16[64,16,512]{2,1,0:T(8,128)(2,1)S(1)} async-done(((bf16[64,16,512]{2,1,0:T(8,128)(2,1)}), bf16[64,16,512]{2,1,0:T(8,128)(2,1)S(1)}, u32[]{:S(2)}, u32[]{:S(2)}) %all-to-all-start) | async-done | bytes 1048608 | tf_op jit(solution)/shard_map/all_to_all | solution.py:371
  38.5 0.0 copy-start.1
  38.5 5.7 %shard_map.160 = bf16[2,64,16,256]{3,2,1,0:T(8,128)(2,1)S(1)} custom-call(bf16[64,16,512]{2,1,0:T(8,128)(2,1)S(1)} %all-to-all-done.x_ref, bf16[512,512]{1,0:T(8,128)(2,1)S(1)} %get-tuple-element.11.d_first_ref, bf16[512,512]{1,0:T(8,128)(2,1)S(1)} %get-tuple-element.12.d_ref, bf16[512,256]{1,0:T(8,128)(2,1)S(1)} %get-tuple-element.13.tc_ref, ...), custom_call_target="tpu_custom_call" | custom-call | tf_op jit(solution)/shard_map/pallas_call | solution.py:348
  44.2 0.0 copy-start
  44.2 0.0 copy-start.2
  44.2 24.3 %all_to_all.10 = bf16[128,16,256]{2,1,0:T(8,128)(2,1)S(1)} all-to-all(bf16[128,16,256]{2,1,0:T(8,128)(2,1)S(1)} %bitcast.7), channel_id=1, replica_groups=mesh['dir'=2,'shard'=64] {'dir','shard'}, dimensions={0} | all-to-all | bytes 2097152 | tf_op jit(solution)/shard_map/all_to_all | solution.py:387
  68.5 0.0 copy-done.1
  68.5 0.0 copy-done
  68.5 0.0 copy-done.2
  68.5 1.2 %shard_map.162 = f32[8,512]{1,0:T(8,128)S(1)} custom-call(bf16[2,1024,256]{2,1,0:T(8,128)(2,1)S(1)} %bitcast.5, bf16[768,128]{1,0:T(8,128)(2,1)S(1)} %copy-done.1, f32[1,1024]{1,0:T(1,128)S(1)} %copy-done.2, bf16[1024,1024]{1,0:T(8,128)(2,1)S(1)} %copy-done), custom_call_target="tpu_custom_call" | custom-call | tf_op jit(solution)/shard_map/pallas_call | solution.py:348
  69.7 0.3 collective-permute-start
  70.0 1.2 %shard_map.161.keep_ref = f32[8,512]{1,0:T(8,128)S(1)} custom-call(bf16[2,1024,256]{2,1,0:T(8,128)(2,1)S(1)} %bitcast.6, bf16[768,128]{1,0:T(8,128)(2,1)S(1)} %copy-done.1, f32[1,1024]{1,0:T(1,128)S(1)} %copy-done.2, bf16[1024,1024]{1,0:T(8,128)(2,1)S(1)} %copy-done), custom_call_target="tpu_custom_call" | custom-call | tf_op jit(solution)/shard_map/pallas_call | solution.py:348
  71.2 2.3 %collective-permute-done.got_ref = f32[8,512]{1,0:T(8,128)S(1)} collective-permute-done((f32[8,512]{1,0:T(8,128)S(1)}, f32[8,512]{1,0:T(8,128)S(1)}, u32[]{:S(2)}, u32[]{:S(2)}) %collective-permute-start) | collective-permute-done | bytes 16416 | tf_op jit(solution)/shard_map/ppermute | solution.py:392
  73.5 0.6 shard_map.163
Async XLA Ops:
  8.7 11.7 %copy-start.4 = (f32[441]{0:T(512)S(1)}, f32[441]{0:T(512)}, u32[]{:S(2)}) copy-start(f32[441]{0:T(512)} %param.21) | copy-start | bytes 5296
  8.7 12.5 %copy-start.3 = (bf16[512,441]{0,1:T(8,128)(2,1)S(1)}, bf16[512,441]{0,1:T(8,128)(2,1)}, u32[]{:S(2)}) copy-start(bf16[512,441]{0,1:T(8,128)(2,1)} %param.20) | copy-start | bytes 1354756
  8.8 29.7 %all-to-all-start = ((bf16[64,16,512]{2,1,0:T(8,128)(2,1)}), bf16[64,16,512]{2,1,0:T(8,128)(2,1)S(1)}, u32[]{:S(2)}, u32[]{:S(2)}) async-start(bf16[64,16,512]{2,1,0:T(8,128)(2,1)} %shard_map.158), calls=%async_computation | async-start | bytes 2097152 | tf_op jit(solution)/shard_map/all_to_all | solution.py:371
  38.5 30.0 %copy-start.1 = (bf16[768,128]{1,0:T(8,128)(2,1)S(1)}, bf16[768,128]{1,0:T(8,128)(2,1)}, u32[]{:S(2)}) copy-start(bf16[768,128]{1,0:T(8,128)(2,1)} %get-tuple-element.17.g_ref) | copy-start | bytes 589828
  44.2 24.3 %copy-start = (bf16[1024,1024]{1,0:T(8,128)(2,1)S(1)}, bf16[1024,1024]{1,0:T(8,128)(2,1)}, u32[]{:S(2)}) copy-start(bf16[1024,1024]{1,0:T(8,128)(2,1)} %get-tuple-element.19.inv_ref) | copy-start | bytes 6291460
  44.2 24.3 %copy-start.2 = (f32[1,1024]{1,0:T(1,128)S(1)}, f32[1,1024]{1,0:T(1,128)}, u32[]{:S(2)}) copy-start(f32[1,1024]{1,0:T(1,128)} %get-tuple-element.18.damp_ref) | copy-start | bytes 12292
  69.7 3.8 %collective-permute-start = (f32[8,512]{1,0:T(8,128)S(1)}, f32[8,512]{1,0:T(8,128)S(1)}, u32[]{:S(2)}, u32[]{:S(2)}) collective-permute-start(f32[8,512]{1,0:T(8,128)S(1)} %shard_map.162), channel_id=1, source_target_pairs={{0,64},{64,0},{1,65},{65,1},{2,66},{66,2},{3,67},{67,3},{4,68},{68... | collective-permute-start | bytes 49160 | tf_op jit(solution)/shard_map/ppermute | solution.py:392

commit v3 on v2

--- a/solution.py
+++ b/solution.py
@@ -91,8 +91,7 @@
         forward=half(forward.reshape(64, 2, 8, CELLS).transpose(1, 0, 2, 3).reshape(1024, CELLS)),
         waves=waves.transpose(0, 2, 1, 3).reshape(8, 1024),
         groups=groups,
-        fx=fx.astype(np.float32),
-        fxp=fx_partner.astype(np.float32),
+        fx=np.stack([fx, fx_partner]).astype(np.float32),
         fxi=half(np.tile(fx_inv.T, (4, 1))),
         inv_x=half(inv_x.reshape(1024, 1024)),
         fx8=half(np.concatenate([np.kron(eye4, fx), np.kron(eye4, fx_partner)], 1)),
@@ -135,15 +134,23 @@
 
 
 def step_one_kernel(
-    orient_ref, waves_ref, fx_ref, fxp_ref, fxi_ref, q_hbm, fwd_hbm, field_hbm,
-    out_hbm, q_ref, fwd_ref, field_ref, turned_ref, moved_ref, out_ref, sems,
+    orient_hbm, waves_hbm, fx_hbm, fxi_hbm, q_hbm, fwd_hbm, field_hbm, out_hbm,
+    orient_ref, waves_ref, fx_ref, fxi_ref, q_ref, fwd_ref, field_ref, turned_ref, moved_ref, out_ref, sems,
 ):
     order = [pl.ds(at, 256) for at in (0, 512, 256, 768)]
     copies = [pltpu.make_async_copy(q_hbm, q_ref, sems.at[4])]
     copies += [pltpu.make_async_copy(fwd_hbm.at[at], fwd_ref.at[at], sems.at[i]) for i, at in enumerate(order)]
     copies += [pltpu.make_async_copy(field_hbm, field_ref, sems.at[5])]
-    for copy in copies[:3]:
+    small = [
+        pltpu.make_async_copy(src, dst, sems.at[10 + i])
+        for i, (src, dst) in enumerate(
+            [(orient_hbm, orient_ref), (waves_hbm, waves_ref), (fx_hbm, fx_ref), (fxi_hbm, fxi_ref)]
+        )
+    ]
+    for copy in small + copies:
         copy.start()
+    for copy in small:
+        copy.wait()
     mine = lax.axis_index("shard") * LOCAL + lax.broadcasted_iota(jnp.int32, (8, 512), 0)
     chosen = (lax.broadcasted_iota(jnp.int32, (8, 512), 1) == mine).astype(F32) * direction_scale()
     hx, hy, hz = [jnp.sum(chosen * orient_ref[i : i + 1, :], 1, keepdims=True) for i in range(3)]
@@ -165,7 +172,7 @@
     twice = jnp.concatenate([fxi_ref[...]] * 2, 1)
     shift_x = []
     for i in range(2):
-        rows = [fx_ref[...] * cx[m : m + 1] + fxp_ref[...] * sx[m : m + 1] for m in range(4 * i, 4 * i + 4)]
+        rows = [fx_ref[0] * cx[m : m + 1] + fx_ref[1] * sx[m : m + 1] for m in range(4 * i, 4 * i + 4)]
         rows2 = jnp.concatenate(split2(jnp.concatenate(rows, 0)), 1)
         shift_x.append(jnp.where(same, dot_nt(twice, rows2), 0.0).astype(BF))
     nyq_x = jnp.where(same, jnp.where((iota_r + iota_c) % 2 == 1, 1.0 / 64, -1.0 / 64), 0.0).astype(BF)
@@ -182,24 +189,23 @@
         return jnp.concatenate(out_re, 0), jnp.concatenate(out_im, 0)
 
     copies[0].wait()
+    spec = []
     for block in range(2):
         at = block * 256
         copies[1 + 2 * block].wait()
         copies[2 + 2 * block].wait()
-        if block == 0:
-            for copy in copies[3:]:
-                copy.start()
-        re = dot_nt(q_ref[...], fwd_ref[at : at + 256, :])
-        im = dot_nt(q_ref[...], fwd_ref[512 + at : 768 + at, :])
+        spec.append([dot_nt(q_ref[...], fwd_ref[row : row + 256, :]) for row in (at, at + 512)])
+    for block in range(2):
+        at = block * 256
+        re, im = spec[block]
         u = rotate(re, im, plain, at, 256)
+        extra = rotate(re[:, 128:], im[:, 128:], tail, 384, 128) if block == 1 else None
         for part in range(2):
             for i in range(2):
                 rows = slice(i * 256, i * 256 + 256)
                 done = dot(shift_x[i], u[part][rows])
                 lanes = part * 512 + at
                 if block == 1:
-                    if i == 0:
-                        extra = rotate(re[:, 128:], im[:, 128:], tail, 384, 128)
                     turned_ref[rows, lanes : lanes + 128] = done[:, :128].astype(BF)
                     more = done[:, 128:] + dot(nyq_x, extra[part][rows])
                     turned_ref[rows, lanes + 128 : lanes + 256] = more.astype(BF)
@@ -284,9 +290,9 @@
                 mixed_ref[pl.ds(2 * quad * 64, 64), pl.ds(pair * 128, 128)] = even.astype(BF)
                 mixed_ref[pl.ds((2 * quad + 1) * 64, 64), pl.ds(pair * 128, 128)] = odd.astype(BF)
 
+    copies[0].wait()
     arrange(0)
     arrange(2)
-    copies[0].wait()
     src = lax.broadcasted_iota(jnp.int32, (256, 256), 0) % 128
     dst = lax.broadcasted_iota(jnp.int32, (256, 256), 1)
     cx = jnp.concatenate([cx_ref[...]] * 2, 1)
@@ -311,11 +317,10 @@
         re, im = turn(at), turn(at + 512)
         turned_ref[:, at : at + 256] = (a * re + b * im).astype(BF)
         turned_ref[:, at + 512 : at + 768] = (d * im - b * re).astype(BF)
+    copies[1].wait()
+    last_ref[...] = dot(d_ref[...], turned_ref[...]).astype(BF)
     for part in range(2):
         at = part * 256
-        last_ref[at : at + 256, :] = dot(d_ref[at : at + 256, :], turned_ref[...]).astype(BF)
-        if part == 0:
-            copies[1].wait()
         out = dot_nt(fxi_ref[...], last_ref[at : at + 256, :]).astype(BF)
         out_ref[part] = out.reshape(64, 16, 256)
 
@@ -362,10 +367,10 @@
     first = call(
         step_one_kernel,
         sds((64, 16, 512), BF),
-        (orient, tab["waves"], tab["fx"], tab["fxp"], tab["fxi"], state, tab["forward"], field),
-        (5, 6, 7),
-        (vm((512, 1024), BF), vm((1024, 1024), BF), vm((64, 1024), F32), vm((512, 1024), BF), vm((512, 1024), BF),
-         vm((64, 16, 512), BF), pltpu.SemaphoreType.DMA((10,))),
+        (orient, tab["waves"], tab["fx"], tab["fxi"], state, tab["forward"], field),
+        range(7),
+        (vm((3, 512), F32), vm((8, 1024), F32), vm((2, 64, 64), F32), vm((256, 64), BF), vm((512, 1024), BF), vm((1024, 1024), BF), vm((64, 1024), F32), vm((512, 1024), BF), vm((512, 1024), BF),
+         vm((64, 16, 512), BF), pltpu.SemaphoreType.DMA((14,))),
         hbm_out=True,
     )
     gathered = lax.all_to_all(first, "shard", split_axis=0, concat_axis=0, tiled=True)

time: 74.4 us -> 72.8 us (0.978)
  Pallas kernels: 21.6 us -> 20.1 us
    pallas_call x6, Pallas kernels: 21.6 us -> 20.1 us  [call(): pl.pallas_call(kernel, out_shape=out_shape, in_specs=[pl.BlockSpec(memory...]
  transfers between devices with their start and end apart: 2 -> 2, of which waited for: 2 -> 2; matrix products, arithmetic and copies ran while one was open for 2% -> 3% of each run, Pallas kernels for 8% -> 8%
where the time goes in v3:
time: 72.8 us; the launch traced here: 72.5 us
  blocking collectives  24.3 us (33%)
  Pallas kernels  20.1 us (28%)
  waiting for transfers between devices  13.6 us (19%)
  starting transfers between devices  11.9 us (16%)
  local copies, waits for them, and re-layouts  1.86 us (3%)
    all_to_all x1, blocking collectives, on_device(): lax.all_to_all(mixed.reshape(128, 16, 256), ('dir', 'shard'), split_axis=...  24.3 us
    pallas_call x6, Pallas kernels, call(): pl.pallas_call(kernel, out_shape=out_shape, in_specs=[pl.BlockSpec(memory...  20.1 us
    all_to_all x1, starting transfers between devices, on_device(): lax.all_to_all(first, 'shard', split_axis=0, concat_axis=0, tiled=True)  11.6 us
    all_to_all x1, waiting for transfers between devices, on_device(): lax.all_to_all(first, 'shard', split_axis=0, concat_axis=0, tiled=True)  11.3 us
    ppermute x1, waiting for transfers between devices, on_device(): got = lax.ppermute(send, 'dir', [(0, 1), (1, 0)])  2.3 us
  transfers between devices with their start and end apart: 2, of which 2 were waited for; matrix products, arithmetic and copies ran while one was open for 3% of the time, Pallas kernels for 8%

profile of v3, /device:TPU:0, one launch (start us, length us, event | category | flops | bytes accessed | tf_op | source)
XLA Modules:
  0.0 72.5 jit_solution(8547201523411273538)
XLA Ops:
  0.6 6.9 %shard_map.149 = bf16[64,16,512]{2,1,0:T(8,128)(2,1)} custom-call(f32[3,512]{1,0:T(4,128)} %orient_ref.1, f32[8,1024]{1,0:T(8,128)} %constant.15.clone.waves_hbm, f32[2,64,64]{2,1,0:T(8,128)} %constant.17.clone.fx_hbm, bf16[256,64]{1,0:T(8,128)(2,1)} %constant.18.clone.fxi_hbm, bf16[512,1024]{1,0:T(8,128)(2,1)} %bitcast.8, ...), custom_call_target="tpu_custom_call" | custom-call | tf_op jit(solution)/shard_map/pallas_call | solution.py:353
  7.6 0.0 copy-start.4
  7.6 0.0 copy-start.3
  7.6 11.6 %all-to-all-start = ((bf16[64,16,512]{2,1,0:T(8,128)(2,1)}), bf16[64,16,512]{2,1,0:T(8,128)(2,1)S(1)}, u32[]{:S(2)}, u32[]{:S(2)}) async-start(bf16[64,16,512]{2,1,0:T(8,128)(2,1)} %shard_map.149), calls=%async_computation | async-start | bytes 2097152 | tf_op jit(solution)/shard_map/all_to_all | solution.py:376
  19.2 0.0 copy-done.4
  19.3 0.8 %copy.18.decay_ref = f32[441,1]{1,0:T(8,128)} copy(f32[441,1]{0,1:T(1,128)S(1)} %bitcast.10) | data formatting | bytes 3528 | tf_op jit(solution)/shard_map/broadcast_in_dim | solution.py:382
  20.1 0.0 copy-done.3
  20.1 1.0 %copy.17.synthesis_ref = bf16[512,441]{1,0:T(8,128)(2,1)} copy(bf16[512,441]{0,1:T(8,128)(2,1)S(1)} %copy-done.3) | data formatting | bytes 903168 | tf_op args[5]
  21.1 4.9 %shard_map.150 = (bf16[512,512]{1,0:T(8,128)(2,1)S(1)}, bf16[512,512]{1,0:T(8,128)(2,1)S(1)}, bf16[512,256]{1,0:T(8,128)(2,1)S(1)}, bf16[512,256]{1,0:T(8,128)(2...) custom-call(f32[3,512]{1,0:T(4,128)} %orient_ref.1, ...), custom_call_target="tpu_custom_call" | custom-call | tf_op jit(solution)/shard_map/pallas_call | solution.py:353
  26.0 11.3 %all-to-all-done.x_ref = bf16[64,16,512]{2,1,0:T(8,128)(2,1)S(1)} async-done(((bf16[64,16,512]{2,1,0:T(8,128)(2,1)}), bf16[64,16,512]{2,1,0:T(8,128)(2,1)S(1)}, u32[]{:S(2)}, u32[]{:S(2)}) %all-to-all-start) | async-done | bytes 1048608 | tf_op jit(solution)/shard_map/all_to_all | solution.py:376
  37.3 0.0 copy-start.1
  37.3 5.2 %shard_map.151 = bf16[2,64,16,256]{3,2,1,0:T(8,128)(2,1)S(1)} custom-call(bf16[64,16,512]{2,1,0:T(8,128)(2,1)S(1)} %all-to-all-done.x_ref, bf16[512,512]{1,0:T(8,128)(2,1)S(1)} %get-tuple-element.11.d_first_ref, bf16[512,512]{1,0:T(8,128)(2,1)S(1)} %get-tuple-element.12.d_ref, bf16[512,256]{1,0:T(8,128)(2,1)S(1)} %get-tuple-element.13.tc_ref, ...), custom_call_target="tpu_custom_call" | custom-call | tf_op jit(solution)/shard_map/pallas_call | solution.py:353
  42.6 0.0 copy-start
  42.6 0.0 copy-start.2
  42.6 24.3 %all_to_all.10 = bf16[128,16,256]{2,1,0:T(8,128)(2,1)S(1)} all-to-all(bf16[128,16,256]{2,1,0:T(8,128)(2,1)S(1)} %bitcast.7), channel_id=1, replica_groups=mesh['dir'=2,'shard'=64] {'dir','shard'}, dimensions={0} | all-to-all | bytes 2097152 | tf_op jit(solution)/shard_map/all_to_all | solution.py:392
  66.9 0.0 copy-done.1
  66.9 0.0 copy-done
  66.9 0.0 copy-done.2
  66.9 1.2 %shard_map.153 = f32[8,512]{1,0:T(8,128)S(1)} custom-call(bf16[2,1024,256]{2,1,0:T(8,128)(2,1)S(1)} %bitcast.5, bf16[768,128]{1,0:T(8,128)(2,1)S(1)} %copy-done.1, f32[1,1024]{1,0:T(1,128)S(1)} %copy-done.2, bf16[1024,1024]{1,0:T(8,128)(2,1)S(1)} %copy-done), custom_call_target="tpu_custom_call" | custom-call | tf_op jit(solution)/shard_map/pallas_call | solution.py:353
  68.1 0.3 collective-permute-start
  68.4 1.2 %shard_map.152.keep_ref = f32[8,512]{1,0:T(8,128)S(1)} custom-call(bf16[2,1024,256]{2,1,0:T(8,128)(2,1)S(1)} %bitcast.6, bf16[768,128]{1,0:T(8,128)(2,1)S(1)} %copy-done.1, f32[1,1024]{1,0:T(1,128)S(1)} %copy-done.2, bf16[1024,1024]{1,0:T(8,128)(2,1)S(1)} %copy-done), custom_call_target="tpu_custom_call" | custom-call | tf_op jit(solution)/shard_map/pallas_call | solution.py:353
  69.6 2.3 %collective-permute-done.got_ref = f32[8,512]{1,0:T(8,128)S(1)} collective-permute-done((f32[8,512]{1,0:T(8,128)S(1)}, f32[8,512]{1,0:T(8,128)S(1)}, u32[]{:S(2)}, u32[]{:S(2)}) %collective-permute-start) | collective-permute-done | bytes 16416 | tf_op jit(solution)/shard_map/ppermute | solution.py:397
  71.9 0.6 shard_map.154
Async XLA Ops:
  7.6 11.7 %copy-start.4 = (f32[441]{0:T(512)S(1)}, f32[441]{0:T(512)}, u32[]{:S(2)}) copy-start(f32[441]{0:T(512)} %param.20) | copy-start | bytes 5296
  7.6 12.5 %copy-start.3 = (bf16[512,441]{0,1:T(8,128)(2,1)S(1)}, bf16[512,441]{0,1:T(8,128)(2,1)}, u32[]{:S(2)}) copy-start(bf16[512,441]{0,1:T(8,128)(2,1)} %param.19) | copy-start | bytes 1354756
  7.6 29.7 %all-to-all-start = ((bf16[64,16,512]{2,1,0:T(8,128)(2,1)}), bf16[64,16,512]{2,1,0:T(8,128)(2,1)S(1)}, u32[]{:S(2)}, u32[]{:S(2)}) async-start(bf16[64,16,512]{2,1,0:T(8,128)(2,1)} %shard_map.149), calls=%async_computation | async-start | bytes 2097152 | tf_op jit(solution)/shard_map/all_to_all | solution.py:376
  37.3 29.6 %copy-start.1 = (bf16[768,128]{1,0:T(8,128)(2,1)S(1)}, bf16[768,128]{1,0:T(8,128)(2,1)}, u32[]{:S(2)}) copy-start(bf16[768,128]{1,0:T(8,128)(2,1)} %get-tuple-element.17.g_ref) | copy-start | bytes 589828
  42.6 24.3 %copy-start = (bf16[1024,1024]{1,0:T(8,128)(2,1)S(1)}, bf16[1024,1024]{1,0:T(8,128)(2,1)}, u32[]{:S(2)}) copy-start(bf16[1024,1024]{1,0:T(8,128)(2,1)} %get-tuple-element.19.inv_ref) | copy-start | bytes 6291460
  42.6 24.3 %copy-start.2 = (f32[1,1024]{1,0:T(1,128)S(1)}, f32[1,1024]{1,0:T(1,128)}, u32[]{:S(2)}) copy-start(f32[1,1024]{1,0:T(1,128)} %get-tuple-element.18.damp_ref) | copy-start | bytes 12292
  68.1 3.8 %collective-permute-start = (f32[8,512]{1,0:T(8,128)S(1)}, f32[8,512]{1,0:T(8,128)S(1)}, u32[]{:S(2)}, u32[]{:S(2)}) collective-permute-start(f32[8,512]{1,0:T(8,128)S(1)} %shard_map.153), channel_id=1, source_target_pairs={{0,64},{64,0},{1,65},{65,1},{2,66},{66,2},{3,67},{67,3},{4,68},{68... | collective-permute-start | bytes 49160 | tf_op jit(solution)/shard_map/ppermute | solution.py:397

commit v4 on v3

--- a/solution.py
+++ b/solution.py
@@ -129,6 +129,14 @@
     return hi, lo
 
 
+CHIPS = ("xh", "y", "z", "core")
+
+
+def shard_index():
+    at = lax.axis_index
+    return ((at("xh") * 4 + at("y")) * 4 + at("z")) * 2 + at("core")
+
+
 def direction_scale():
     return TRANSPORT * (1.0 - 2.0 * lax.axis_index("dir").astype(F32))
 
@@ -151,7 +159,7 @@
         copy.start()
     for copy in small:
         copy.wait()
-    mine = lax.axis_index("shard") * LOCAL + lax.broadcasted_iota(jnp.int32, (8, 512), 0)
+    mine = shard_index() * LOCAL + lax.broadcasted_iota(jnp.int32, (8, 512), 0)
     chosen = (lax.broadcasted_iota(jnp.int32, (8, 512), 1) == mine).astype(F32) * direction_scale()
     hx, hy, hz = [jnp.sum(chosen * orient_ref[i : i + 1, :], 1, keepdims=True) for i in range(3)]
     w = waves_ref[...]
@@ -244,7 +252,7 @@
     g = jnp.concatenate([g, jnp.zeros((120, 256), F32)], 0).T
     g_hi, g_lo = split2(g)
     g_ref[...] = jnp.concatenate([g_hi, g_hi, g_lo], 0)
-    damp = jnp.exp(-field_ref[pl.ds(lax.axis_index("shard"), 1), :])
+    damp = jnp.exp(-field_ref[pl.ds(shard_index(), 1), :])
     damp_ref[...] = damp * damp
     inv_ref[...] = fwd_ref[...].T
     scaled = (analysis_ref[...].astype(F32) * decay_ref[...]).astype(BF)
@@ -261,7 +269,7 @@
     is_nyq = lane == 32
     cx_ref[...] = jnp.where(is_nyq, 1.0, turns_cos(hx * freq))
     sx_ref[...] = jnp.where(is_nyq, 0.0, turns_sin(hx * freq))
-    w = groups_ref[lax.axis_index("shard")]
+    w = groups_ref[shard_index()]
     rest = hy * w[0:1] + hz * w[1:2]
     cn = turns_cos(hx * w[4:5] + hy * w[2:3] + hz * w[3:4]) * w[5:6]
     tc_ref[...] = jnp.concatenate(split2(turns_cos(rest) * cn), 1)
@@ -322,14 +330,17 @@
     for part in range(2):
         at = part * 256
         out = dot_nt(fxi_ref[...], last_ref[at : at + 256, :]).astype(BF)
-        out_ref[part] = out.reshape(64, 16, 256)
+        out = out.reshape(32, 2, 16, 256)
+        for core in range(2):
+            out_ref[core, part] = out[:, core]
 
 
 def moment_kernel(own, x_ref, g_ref, damp_ref, inv_ref, out_ref):
     me = lax.axis_index("dir")
     base = pl.multiple_of((me if own else 1 - me) * 512, 512)
-    x = x_ref[...].reshape(2, 64, 2, 8, 256)
-    x = [jnp.concatenate([x[p, :, 0].reshape(512, 256), x[p, :, 1].reshape(512, 256)], 0) for p in range(2)]
+    x = x_ref[...].reshape(2, 2, 32, 2, 8, 256)
+    rows = lambda p, part: jnp.stack([x[0, p, :, part], x[1, p, :, part]], 1).reshape(512, 256)
+    x = [jnp.concatenate([rows(p, 0), rows(p, 1)], 0) for p in range(2)]
     parts = []
     for block in range(2):
         inv = inv_ref[pl.ds(base + block * 256, 256), :]
@@ -373,7 +384,7 @@
          vm((64, 16, 512), BF), pltpu.SemaphoreType.DMA((14,))),
         hbm_out=True,
     )
-    gathered = lax.all_to_all(first, "shard", split_axis=0, concat_axis=0, tiled=True)
+    gathered = lax.all_to_all(first, CHIPS, split_axis=0, concat_axis=0, tiled=True)
     *prepared, inverse, g, damp = call(
         prepare_kernel,
         (vm((512, 512), BF), vm((512, 512), BF), vm((512, 256), BF), vm((512, 256), BF),
@@ -383,15 +394,15 @@
     )
     mixed = call(
         mix_kernel,
-        vm((2, 64, 16, 256), BF),
+        vm((2, 2, 32, 16, 256), BF),
         tuple(on_chip(v) for v in (gathered, *prepared)) + (tab["fx8"], tab["inv_x"]),
         (7, 8),
         (vm((4, 1024, 128), F32), vm((512, 1024), BF), vm((512, 1024), BF), vm((512, 1024), BF), vm((256, 512), BF),
          vm((1024, 1024), BF), pltpu.SemaphoreType.DMA((2,))),
     )
     planes = lax.all_to_all(
-        mixed.reshape(128, 16, 256), ("dir", "shard"), split_axis=0, concat_axis=0, tiled=True
-    ).reshape(2, 1024, 256)
+        mixed.reshape(128, 16, 256), ("core", "dir", "xh", "y", "z"), split_axis=0, concat_axis=0, tiled=True
+    )
     operands = tuple(on_chip(v) for v in (planes, g, damp, inverse))
     send = call(functools.partial(moment_kernel, False), vm((8, 512), F32), operands)
     got = lax.ppermute(send, "dir", [(0, 1), (1, 0)])
@@ -401,6 +412,7 @@
 
 
 def solution(mesh):
-    in_specs = (P("dir", "shard", None, None), P(), P(), P(), P(), P(), P())
-    out_specs = (P("shard", "dir"), P(None, "shard", "dir"))
-    return jax.shard_map(on_device, mesh=mesh, in_specs=in_specs, out_specs=out_specs, check_vma=False)
+    fine = jax.sharding.Mesh(mesh.devices.reshape(2, 2, 4, 4, 2), ("dir",) + CHIPS)
+    in_specs = (P("dir", CHIPS, None, None), P(), P(), P(), P(), P(), P())
+    out_specs = (P(CHIPS, "dir"), P(None, CHIPS, "dir"))
+    return jax.shard_map(on_device, mesh=fine, in_specs=in_specs, out_specs=out_specs, check_vma=False)

time: 72.8 us -> 71.9 us (0.988)
  blocking collectives: 24.3 us -> 23.1 us
    all_to_all x1, blocking collectives: 24.3 us -> 23.1 us  [on_device(): lax.all_to_all(mixed.reshape(128, 16, 256), ('core', 'dir', 'xh', 'y', 'z...]
  transfers between devices with their start and end apart: 2 -> 2, of which waited for: 2 -> 2; matrix products, arithmetic and copies ran while one was open for 3% -> 3% of each run, Pallas kernels for 8% -> 9%
where the time goes in v4:
time: 71.9 us; the launch traced here: 71.3 us
  blocking collectives  23.1 us (32%)
  Pallas kernels  20 us (28%)
  waiting for transfers between devices  13.3 us (18%)
  starting transfers between devices  12.3 us (17%)
  local copies, waits for them, and re-layouts  1.86 us (3%)
    all_to_all x1, blocking collectives, on_device(): lax.all_to_all(mixed.reshape(128, 16, 256), ('core', 'dir', 'xh', 'y', 'z...  23.1 us
    pallas_call x6, Pallas kernels, call(): pl.pallas_call(kernel, out_shape=out_shape, in_specs=[pl.BlockSpec(memory...  20 us
    all_to_all x1, starting transfers between devices, on_device(): lax.all_to_all(first, CHIPS, split_axis=0, concat_axis=0, tiled=True)  11.6 us
    all_to_all x1, waiting for transfers between devices, on_device(): lax.all_to_all(first, CHIPS, split_axis=0, concat_axis=0, tiled=True)  11.3 us
    ppermute x1, waiting for transfers between devices, on_device(): got = lax.ppermute(send, 'dir', [(0, 1), (1, 0)])  1.97 us
  transfers between devices with their start and end apart: 2, of which 2 were waited for; matrix products, arithmetic and copies ran while one was open for 3% of the time, Pallas kernels for 9%

profile of v4, /device:TPU:0, one launch (start us, length us, event | category | flops | bytes accessed | tf_op | source)
XLA Modules:
  0.0 71.3 jit_solution(9748076154092964387)
XLA Ops:
  0.6 6.9 %shard_map.149 = bf16[64,16,512]{2,1,0:T(8,128)(2,1)} custom-call(f32[3,512]{1,0:T(4,128)} %orient_ref.1, f32[8,1024]{1,0:T(8,128)} %constant.15.clone.waves_hbm, f32[2,64,64]{2,1,0:T(8,128)} %constant.17.clone.fx_hbm, bf16[256,64]{1,0:T(8,128)(2,1)} %constant.18.clone.fxi_hbm, bf16[512,1024]{1,0:T(8,128)(2,1)} %bitcast.5, ...), custom_call_target="tpu_custom_call" | custom-call | tf_op jit(solution)/shard_map/pallas_call | solution.py:364
  7.6 0.0 copy-start.4
  7.6 0.0 copy-start.3
  7.6 11.6 %all-to-all-start = ((bf16[64,16,512]{2,1,0:T(8,128)(2,1)}), bf16[64,16,512]{2,1,0:T(8,128)(2,1)S(1)}, u32[]{:S(2)}, u32[]{:S(2)}) async-start(bf16[64,16,512]{2,1,0:T(8,128)(2,1)} %shard_map.149), calls=%async_computation | async-start | bytes 2097152 | tf_op jit(solution)/shard_map/all_to_all | solution.py:387
  19.2 0.0 copy-done.4
  19.3 0.8 %copy.18.decay_ref = f32[441,1]{1,0:T(8,128)} copy(f32[441,1]{0,1:T(1,128)S(1)} %bitcast.7) | data formatting | bytes 3528 | tf_op jit(solution)/shard_map/broadcast_in_dim | solution.py:393
  20.1 0.0 copy-done.3
  20.1 1.0 %copy.17.synthesis_ref = bf16[512,441]{1,0:T(8,128)(2,1)} copy(bf16[512,441]{0,1:T(8,128)(2,1)S(1)} %copy-done.3) | data formatting | bytes 903168 | tf_op args[5]
  21.1 4.9 %shard_map.150 = (bf16[512,512]{1,0:T(8,128)(2,1)S(1)}, bf16[512,512]{1,0:T(8,128)(2,1)S(1)}, bf16[512,256]{1,0:T(8,128)(2,1)S(1)}, bf16[512,256]{1,0:T(8,128)(2...) custom-call(f32[3,512]{1,0:T(4,128)} %orient_ref.1, ...), custom_call_target="tpu_custom_call" | custom-call | tf_op jit(solution)/shard_map/pallas_call | solution.py:364
  26.0 11.3 %all-to-all-done.x_ref = bf16[64,16,512]{2,1,0:T(8,128)(2,1)S(1)} async-done(((bf16[64,16,512]{2,1,0:T(8,128)(2,1)}), bf16[64,16,512]{2,1,0:T(8,128)(2,1)S(1)}, u32[]{:S(2)}, u32[]{:S(2)}) %all-to-all-start) | async-done | bytes 1048608 | tf_op jit(solution)/shard_map/all_to_all | solution.py:387
  37.3 0.0 copy-start.1
  37.3 5.2 %shard_map.151 = bf16[2,2,32,16,256]{4,3,2,1,0:T(8,128)(2,1)S(1)} custom-call(bf16[64,16,512]{2,1,0:T(8,128)(2,1)S(1)} %all-to-all-done.x_ref, bf16[512,512]{1,0:T(8,128)(2,1)S(1)} %get-tuple-element.11.d_first_ref, bf16[512,512]{1,0:T(8,128)(2,1)S(1)} %get-tuple-element.12.d_ref, bf16[512,256]{1,0:T(8,128)(2,1)S(1)} %get-tuple-element.13.tc_ref, ...), custom_call_target="tpu_custom_call" | custom-call | tf_op jit(solution)/shard_map/pallas_call | solution.py:364
  42.6 0.0 copy-start
  42.6 0.0 copy-start.2
  42.6 23.1 %all_to_all.10.x_ref = bf16[128,16,256]{2,1,0:T(8,128)(2,1)S(1)} all-to-all(bf16[128,16,256]{2,1,0:T(8,128)(2,1)S(1)} %bitcast.4), channel_id=1, replica_groups=mesh['dir'=2,'xh'=2,'y'=4,'z'=4,'core'=2] {'core','dir','xh','y','z'}, dimensions={0} | all-to-all | bytes 2097152 | tf_op jit(solution)/shard_map/all_to_all | solution.py:403
  65.7 0.0 copy-done.1
  65.7 0.0 copy-done
  65.7 0.0 copy-done.2
  65.7 1.2 %shard_map.153 = f32[8,512]{1,0:T(8,128)S(1)} custom-call(bf16[128,16,256]{2,1,0:T(8,128)(2,1)S(1)} %all_to_all.10.x_ref, bf16[768,128]{1,0:T(8,128)(2,1)S(1)} %copy-done.1, f32[1,1024]{1,0:T(1,128)S(1)} %copy-done.2, bf16[1024,1024]{1,0:T(8,128)(2,1)S(1)} %copy-done), custom_call_target="tpu_custom_call" | custom-call | tf_op jit(solution)/shard_map/pallas_call | solution.py:364
  66.9 0.6 collective-permute-start
  67.5 1.2 %shard_map.152.keep_ref = f32[8,512]{1,0:T(8,128)S(1)} custom-call(bf16[128,16,256]{2,1,0:T(8,128)(2,1)S(1)} %all_to_all.10.x_ref, bf16[768,128]{1,0:T(8,128)(2,1)S(1)} %copy-done.1, f32[1,1024]{1,0:T(1,128)S(1)} %copy-done.2, bf16[1024,1024]{1,0:T(8,128)(2,1)S(1)} %copy-done), custom_call_target="tpu_custom_call" | custom-call | tf_op jit(solution)/shard_map/pallas_call | solution.py:364
  68.7 2.0 %collective-permute-done.got_ref = f32[8,512]{1,0:T(8,128)S(1)} collective-permute-done((f32[8,512]{1,0:T(8,128)S(1)}, f32[8,512]{1,0:T(8,128)S(1)}, u32[]{:S(2)}, u32[]{:S(2)}) %collective-permute-start) | collective-permute-done | bytes 16416 | tf_op jit(solution)/shard_map/ppermute | solution.py:408
  70.7 0.6 shard_map.154
Async XLA Ops:
  7.6 11.7 %copy-start.4 = (f32[441]{0:T(512)S(1)}, f32[441]{0:T(512)}, u32[]{:S(2)}) copy-start(f32[441]{0:T(512)} %param.20) | copy-start | bytes 5296
  7.6 12.5 %copy-start.3 = (bf16[512,441]{0,1:T(8,128)(2,1)S(1)}, bf16[512,441]{0,1:T(8,128)(2,1)}, u32[]{:S(2)}) copy-start(bf16[512,441]{0,1:T(8,128)(2,1)} %param.19) | copy-start | bytes 1354756
  7.6 29.7 %all-to-all-start = ((bf16[64,16,512]{2,1,0:T(8,128)(2,1)}), bf16[64,16,512]{2,1,0:T(8,128)(2,1)S(1)}, u32[]{:S(2)}, u32[]{:S(2)}) async-start(bf16[64,16,512]{2,1,0:T(8,128)(2,1)} %shard_map.149), calls=%async_computation | async-start | bytes 2097152 | tf_op jit(solution)/shard_map/all_to_all | solution.py:387
  37.3 28.4 %copy-start.1 = (bf16[768,128]{1,0:T(8,128)(2,1)S(1)}, bf16[768,128]{1,0:T(8,128)(2,1)}, u32[]{:S(2)}) copy-start(bf16[768,128]{1,0:T(8,128)(2,1)} %get-tuple-element.17.g_ref) | copy-start | bytes 589828
  42.6 23.1 %copy-start = (bf16[1024,1024]{1,0:T(8,128)(2,1)S(1)}, bf16[1024,1024]{1,0:T(8,128)(2,1)}, u32[]{:S(2)}) copy-start(bf16[1024,1024]{1,0:T(8,128)(2,1)} %get-tuple-element.19.inv_ref) | copy-start | bytes 6291460
  42.6 23.1 %copy-start.2 = (f32[1,1024]{1,0:T(1,128)S(1)}, f32[1,1024]{1,0:T(1,128)}, u32[]{:S(2)}) copy-start(f32[1,1024]{1,0:T(1,128)} %get-tuple-element.18.damp_ref) | copy-start | bytes 12292
  66.9 3.8 %collective-permute-start = (f32[8,512]{1,0:T(8,128)S(1)}, f32[8,512]{1,0:T(8,128)S(1)}, u32[]{:S(2)}, u32[]{:S(2)}) collective-permute-start(f32[8,512]{1,0:T(8,128)S(1)} %shard_map.153), channel_id=1, source_target_pairs={{0,64},{64,0},{1,65},{65,1},{2,66},{66,2},{3,67},{67,3},{4,68},{68... | collective-permute-start | bytes 49160 | tf_op jit(solution)/shard_map/ppermute | solution.py:408

commit v5 on v4

--- a/solution.py
+++ b/solution.py
@@ -259,7 +259,7 @@
     d_ref[...] = dot(synthesis_ref[...], scaled).astype(BF)
     row = lax.broadcasted_iota(jnp.int32, (512, 512), 0)
     col = lax.broadcasted_iota(jnp.int32, (512, 512), 1)
-    perm = ((row % 8) * 64 + row // 8 == col).astype(BF)
+    perm = ((row % 8) * 64 + (row // 8) % 2 * 32 + row // 16 == col).astype(BF)
     d_first_ref[...] = dot(d_ref[...], perm).astype(BF)
     o = orient_ref[...] * direction_scale()
     head = jnp.concatenate([o, o, o[:2]], 0).T
@@ -269,7 +269,7 @@
     is_nyq = lane == 32
     cx_ref[...] = jnp.where(is_nyq, 1.0, turns_cos(hx * freq))
     sx_ref[...] = jnp.where(is_nyq, 0.0, turns_sin(hx * freq))
-    w = groups_ref[shard_index()]
+    w = groups_ref[lax.axis_index("core") * 32 + shard_index() // 2]
     rest = hy * w[0:1] + hz * w[1:2]
     cn = turns_cos(hx * w[4:5] + hy * w[2:3] + hz * w[3:4]) * w[5:6]
     tc_ref[...] = jnp.concatenate(split2(turns_cos(rest) * cn), 1)
@@ -339,7 +339,7 @@
     me = lax.axis_index("dir")
     base = pl.multiple_of((me if own else 1 - me) * 512, 512)
     x = x_ref[...].reshape(2, 2, 32, 2, 8, 256)
-    rows = lambda p, part: jnp.stack([x[0, p, :, part], x[1, p, :, part]], 1).reshape(512, 256)
+    rows = lambda p, part: jnp.concatenate([x[core, p, :, part].reshape(256, 256) for core in range(2)], 0)
     x = [jnp.concatenate([rows(p, 0), rows(p, 1)], 0) for p in range(2)]
     parts = []
     for block in range(2):
@@ -384,7 +384,7 @@
          vm((64, 16, 512), BF), pltpu.SemaphoreType.DMA((14,))),
         hbm_out=True,
     )
-    gathered = lax.all_to_all(first, CHIPS, split_axis=0, concat_axis=0, tiled=True)
+    gathered = lax.all_to_all(first, ("core", "xh", "y", "z"), split_axis=0, concat_axis=0, tiled=True)
     *prepared, inverse, g, damp = call(
         prepare_kernel,
         (vm((512, 512), BF), vm((512, 512), BF), vm((512, 256), BF), vm((512, 256), BF),

time: 71.9 us -> 71.7 us (level)
  blocking collectives: 23.1 us -> 21.7 us
  waiting for transfers between devices: 13.3 us -> 14.5 us
    all_to_all x1, blocking collectives: 23.1 us -> 21.7 us  [on_device(): lax.all_to_all(mixed.reshape(128, 16, 256), ('core', 'dir', 'xh', 'y', 'z...]
    all_to_all x1, waiting for transfers between devices: 11.3 us -> 12.5 us  [on_device(): lax.all_to_all(first, ('core', 'xh', 'y', 'z'), split_axis=0, concat_axis...]
where the time goes in v5:
time: 71.7 us; the launch traced here: 71.1 us
  blocking collectives  21.7 us (30%)
  Pallas kernels  20.1 us (28%)
  waiting for transfers between devices  14.5 us (20%)
  starting transfers between devices  12.3 us (17%)
  local copies, waits for them, and re-layouts  1.86 us (3%)
    all_to_all x1, blocking collectives, on_device(): lax.all_to_all(mixed.reshape(128, 16, 256), ('core', 'dir', 'xh', 'y', 'z...  21.7 us
    pallas_call x6, Pallas kernels, call(): pl.pallas_call(kernel, out_shape=out_shape, in_specs=[pl.BlockSpec(memory...  20.1 us
    all_to_all x1, waiting for transfers between devices, on_device(): lax.all_to_all(first, ('core', 'xh', 'y', 'z'), split_axis=0, concat_axis...  12.5 us
    all_to_all x1, starting transfers between devices, on_device(): lax.all_to_all(first, ('core', 'xh', 'y', 'z'), split_axis=0, concat_axis...  11.6 us
    ppermute x1, waiting for transfers between devices, on_device(): got = lax.ppermute(send, 'dir', [(0, 1), (1, 0)])  1.98 us
  transfers between devices with their start and end apart: 2, of which 2 were waited for; matrix products, arithmetic and copies ran while one was open for 3% of the time, Pallas kernels for 9%

profile of v5, /device:TPU:0, one launch (start us, length us, event | category | flops | bytes accessed | tf_op | source)
XLA Modules:
  0.0 71.1 jit_solution(14119168455627286482)
XLA Ops:
  0.6 6.9 %shard_map.149 = bf16[64,16,512]{2,1,0:T(8,128)(2,1)} custom-call(f32[3,512]{1,0:T(4,128)} %orient_ref.1, f32[8,1024]{1,0:T(8,128)} %constant.15.clone.waves_hbm, f32[2,64,64]{2,1,0:T(8,128)} %constant.17.clone.fx_hbm, bf16[256,64]{1,0:T(8,128)(2,1)} %constant.18.clone.fxi_hbm, bf16[512,1024]{1,0:T(8,128)(2,1)} %bitcast.5, ...), custom_call_target="tpu_custom_call" | custom-call | tf_op jit(solution)/shard_map/pallas_call | solution.py:364
  7.6 0.0 copy-start.4
  7.6 0.0 copy-start.3
  7.6 11.6 %all-to-all-start = ((bf16[64,16,512]{2,1,0:T(8,128)(2,1)}), bf16[64,16,512]{2,1,0:T(8,128)(2,1)S(1)}, u32[]{:S(2)}, u32[]{:S(2)}) async-start(bf16[64,16,512]{2,1,0:T(8,128)(2,1)} %shard_map.149), calls=%async_computation | async-start | bytes 2097152 | tf_op jit(solution)/shard_map/all_to_all | solution.py:387
  19.2 0.0 copy-done.4
  19.3 0.8 %copy.18.decay_ref = f32[441,1]{1,0:T(8,128)} copy(f32[441,1]{0,1:T(1,128)S(1)} %bitcast.7) | data formatting | bytes 3528 | tf_op jit(solution)/shard_map/broadcast_in_dim | solution.py:393
  20.1 0.0 copy-done.3
  20.1 1.0 %copy.17.synthesis_ref = bf16[512,441]{1,0:T(8,128)(2,1)} copy(bf16[512,441]{0,1:T(8,128)(2,1)S(1)} %copy-done.3) | data formatting | bytes 903168 | tf_op args[5]
  21.1 4.9 %shard_map.150 = (bf16[512,512]{1,0:T(8,128)(2,1)S(1)}, bf16[512,512]{1,0:T(8,128)(2,1)S(1)}, bf16[512,256]{1,0:T(8,128)(2,1)S(1)}, bf16[512,256]{1,0:T(8,128)(2...) custom-call(f32[3,512]{1,0:T(4,128)} %orient_ref.1, ...), custom_call_target="tpu_custom_call" | custom-call | tf_op jit(solution)/shard_map/pallas_call | solution.py:364
  26.0 12.5 %all-to-all-done.x_ref = bf16[64,16,512]{2,1,0:T(8,128)(2,1)S(1)} async-done(((bf16[64,16,512]{2,1,0:T(8,128)(2,1)}), bf16[64,16,512]{2,1,0:T(8,128)(2,1)S(1)}, u32[]{:S(2)}, u32[]{:S(2)}) %all-to-all-start) | async-done | bytes 1048608 | tf_op jit(solution)/shard_map/all_to_all | solution.py:387
  38.5 0.0 copy-start.1
  38.5 5.2 %shard_map.151 = bf16[2,2,32,16,256]{4,3,2,1,0:T(8,128)(2,1)S(1)} custom-call(bf16[64,16,512]{2,1,0:T(8,128)(2,1)S(1)} %all-to-all-done.x_ref, bf16[512,512]{1,0:T(8,128)(2,1)S(1)} %get-tuple-element.11.d_first_ref, bf16[512,512]{1,0:T(8,128)(2,1)S(1)} %get-tuple-element.12.d_ref, bf16[512,256]{1,0:T(8,128)(2,1)S(1)} %get-tuple-element.13.tc_ref, ...), custom_call_target="tpu_custom_call" | custom-call | tf_op jit(solution)/shard_map/pallas_call | solution.py:364
  43.7 0.0 copy-start
  43.7 0.0 copy-start.2
  43.8 21.7 %all_to_all.10.x_ref = bf16[128,16,256]{2,1,0:T(8,128)(2,1)S(1)} all-to-all(bf16[128,16,256]{2,1,0:T(8,128)(2,1)S(1)} %bitcast.4), channel_id=1, replica_groups=mesh['dir'=2,'xh'=2,'y'=4,'z'=4,'core'=2] {'core','dir','xh','y','z'}, dimensions={0} | all-to-all | bytes 2097152 | tf_op jit(solution)/shard_map/all_to_all | solution.py:403
  65.5 0.0 copy-done.1
  65.5 0.0 copy-done
  65.5 0.0 copy-done.2
  65.5 1.2 %shard_map.153 = f32[8,512]{1,0:T(8,128)S(1)} custom-call(bf16[128,16,256]{2,1,0:T(8,128)(2,1)S(1)} %all_to_all.10.x_ref, bf16[768,128]{1,0:T(8,128)(2,1)S(1)} %copy-done.1, f32[1,1024]{1,0:T(1,128)S(1)} %copy-done.2, bf16[1024,1024]{1,0:T(8,128)(2,1)S(1)} %copy-done), custom_call_target="tpu_custom_call" | custom-call | tf_op jit(solution)/shard_map/pallas_call | solution.py:364
  66.7 0.6 collective-permute-start
  67.3 1.2 %shard_map.152.keep_ref = f32[8,512]{1,0:T(8,128)S(1)} custom-call(bf16[128,16,256]{2,1,0:T(8,128)(2,1)S(1)} %all_to_all.10.x_ref, bf16[768,128]{1,0:T(8,128)(2,1)S(1)} %copy-done.1, f32[1,1024]{1,0:T(1,128)S(1)} %copy-done.2, bf16[1024,1024]{1,0:T(8,128)(2,1)S(1)} %copy-done), custom_call_target="tpu_custom_call" | custom-call | tf_op jit(solution)/shard_map/pallas_call | solution.py:364
  68.5 2.0 %collective-permute-done.got_ref = f32[8,512]{1,0:T(8,128)S(1)} collective-permute-done((f32[8,512]{1,0:T(8,128)S(1)}, f32[8,512]{1,0:T(8,128)S(1)}, u32[]{:S(2)}, u32[]{:S(2)}) %collective-permute-start) | collective-permute-done | bytes 16416 | tf_op jit(solution)/shard_map/ppermute | solution.py:408
  70.5 0.6 shard_map.154
Async XLA Ops:
  7.6 11.7 %copy-start.4 = (f32[441]{0:T(512)S(1)}, f32[441]{0:T(512)}, u32[]{:S(2)}) copy-start(f32[441]{0:T(512)} %param.20) | copy-start | bytes 5296
  7.6 12.5 %copy-start.3 = (bf16[512,441]{0,1:T(8,128)(2,1)S(1)}, bf16[512,441]{0,1:T(8,128)(2,1)}, u32[]{:S(2)}) copy-start(bf16[512,441]{0,1:T(8,128)(2,1)} %param.19) | copy-start | bytes 1354756
  7.6 30.9 %all-to-all-start = ((bf16[64,16,512]{2,1,0:T(8,128)(2,1)}), bf16[64,16,512]{2,1,0:T(8,128)(2,1)S(1)}, u32[]{:S(2)}, u32[]{:S(2)}) async-start(bf16[64,16,512]{2,1,0:T(8,128)(2,1)} %shard_map.149), calls=%async_computation | async-start | bytes 2097152 | tf_op jit(solution)/shard_map/all_to_all | solution.py:387
  38.5 27.0 %copy-start.1 = (bf16[768,128]{1,0:T(8,128)(2,1)S(1)}, bf16[768,128]{1,0:T(8,128)(2,1)}, u32[]{:S(2)}) copy-start(bf16[768,128]{1,0:T(8,128)(2,1)} %get-tuple-element.17.g_ref) | copy-start | bytes 589828
  43.7 21.7 %copy-start = (bf16[1024,1024]{1,0:T(8,128)(2,1)S(1)}, bf16[1024,1024]{1,0:T(8,128)(2,1)}, u32[]{:S(2)}) copy-start(bf16[1024,1024]{1,0:T(8,128)(2,1)} %get-tuple-element.19.inv_ref) | copy-start | bytes 6291460
  43.7 21.7 %copy-start.2 = (f32[1,1024]{1,0:T(1,128)S(1)}, f32[1,1024]{1,0:T(1,128)}, u32[]{:S(2)}) copy-start(f32[1,1024]{1,0:T(1,128)} %get-tuple-element.18.damp_ref) | copy-start | bytes 12292
  66.7 3.8 %collective-permute-start = (f32[8,512]{1,0:T(8,128)S(1)}, f32[8,512]{1,0:T(8,128)S(1)}, u32[]{:S(2)}, u32[]{:S(2)}) collective-permute-start(f32[8,512]{1,0:T(8,128)S(1)} %shard_map.153), channel_id=1, source_target_pairs={{0,64},{64,0},{1,65},{65,1},{2,66},{66,2},{3,67},{67,3},{4,68},{68... | collective-permute-start | bytes 49160 | tf_op jit(solution)/shard_map/ppermute | solution.py:408
